TPU v7x, 512 devices: a whole 4x8x8 slice. The times are simulated.
512 devices in a mesh: lrow: 8 (over z), rcol: 16 (over x, y_lo, core), term: 4 (over y_hi).
Axes of the slice: x: 4, y: 8 (y_hi: 4, y_lo: 2; y = y_hi * 2 + y_lo), z: 8, core: 2. Of those that a mesh axis runs over, the one named last changes fastest.
Arguments:
- core_left: bfloat16 [256, 256, 128], P(None, 'rcol'), may hold values from -6 to 6
- core_right: bfloat16 [256, 256, 128], P('rcol', 'lrow'), may hold values from -0.03125 to 0.03125
- env_left: bfloat16 [20, 32, 256], P('term', 'lrow'), may hold values from -0.375 to 0.375
- env_right: bfloat16 [20, 256, 256], P('term'), may hold values from -0.375 to 0.375
- coef_left: float32 [20, 3, 128], P('term'), may hold values from -1.5 to 1.5
- coef_right: float32 [20, 3, 128], P('term'), may hold values from -1.5 to 1.5
- projected: bfloat16 [128, 32, 256, 128], P('term', 'lrow', 'rcol'), may hold values from -6 to 6
Outputs:
- residual: bfloat16 [128, 32, 256, 128], P('term', 'lrow', 'rcol')
All inputs are finite; a program needn't handle non-finite values.
Results may differ from a plain program's by a relative error of at most 0.012.
Values may be sent and summed in bfloat16 or wider, within the bound.
No kernel may reach another device: no remote copies, remote signals or barrier semaphores. Data moves between devices by JAX's collectives and lax.ppermute only.
A program may use at most 64 MiB of HBM per device.

v0:
```python
import jax
import jax.numpy as jnp
from jax import lax
from jax.sharding import PartitionSpec as P


def stencil_terms(field, coef):
    wide = field.astype(jnp.float32)
    zero = jnp.zeros_like(wide[..., :1])
    before = jnp.concatenate([zero, wide[..., :-1]], axis=-1)
    after = jnp.concatenate([wide[..., 1:], zero], axis=-1)
    scaled = coef[:, :, None, None, :]
    return scaled[:, 0] * wide[None] + scaled[:, 1] * before[None] + scaled[:, 2] * after[None]


def on_device(core_left, core_right, env_left, env_right, coef_left, coef_right, projected):
    left_field = stencil_terms(core_left, coef_left).astype(jnp.bfloat16)
    left_frame = jnp.einsum(
        "tpq,tqrs->trps", env_left, left_field, preferred_element_type=jnp.float32
    ).astype(jnp.bfloat16)
    left_frame = lax.all_gather(left_frame, "rcol", axis=1, tiled=True)
    right_block = lax.all_gather(core_right, "lrow", axis=1, tiled=True)
    right_field = stencil_terms(right_block, coef_right).astype(jnp.bfloat16)
    right_frame = jnp.einsum(
        "tbq,trqj->trbj", env_right, right_field, preferred_element_type=jnp.float32
    ).astype(jnp.bfloat16)
    partial_sum = jnp.einsum(
        "trai,trbj->jabi",
        left_frame,
        lax.all_to_all(right_frame, "rcol", split_axis=2, concat_axis=1, tiled=True),
        preferred_element_type=jnp.float32,
    )
    summed = lax.psum_scatter(
        partial_sum.astype(jnp.bfloat16), "term", scatter_dimension=0, tiled=True
    ).astype(jnp.float32)
    return (projected.astype(jnp.float32) - summed).astype(jnp.bfloat16)


def solution(mesh):
    return jax.shard_map(
        on_device,
        mesh=mesh,
        in_specs=(
            P(None, "rcol", None),
            P("rcol", "lrow", None),
            P("term", "lrow", None),
            P("term", None, None),
            P("term", None, None),
            P("term", None, None),
            P("term", "lrow", "rcol", None),
        ),
        out_specs=P("term", "lrow", "rcol", None),
        check_vma=False,
    )
```

profile of v0, /device:TPU:1, one launch (start us, length us, event | category | flops | bytes accessed | tf_op | source)
XLA Modules:
  0.0 234.9 jit_solution(17720216909429817425)
XLA Ops:
  7.4 0.0 copy-start
  7.4 0.0 all-gather.3.cloned.1.call-start
  7.4 0.7 all-gather.3.cloned.1.call-update
  8.1 0.8 fusion.24
  8.9 44.4 %all-gather.3.cloned.1.call-done = bf16[16,256,128]{2,1,0:T(8,128)(2,1)} async-done(((bf16[16,32,128]{2,1,0:T(8,128)(2,1)}), bf16[16,256,128]{2,1,0:T(8,128)(2,1)}) %all-gather.3.cloned.1.call-update) | async-done | bytes 1048592 | tf_op jit(solution)/shard_map/all_gather | solution.py:22
  53.4 3.4 %fusion.22 = (f32[16,256,127]{2,1,0:T(8,128)}, f32[16,256,127]{2,1,0:T(8,128)S(1)}) fusion(bf16[16,256,128]{2,1,0:T(8,128)(2,1)} %all-gather.3.cloned.1.call-done), kind=kLoop, calls=%fused_computation.29 | loop fusion | bytes 8323072 | tf_op jit(solution)/shard_map/slice | solution.py:10
  56.8 2.9 %copy.48 = f32[16,256,127]{1,2,0:T(8,128)} copy(f32[16,256,127]{2,1,0:T(8,128)} %get-tuple-element.7) | data formatting | bytes 4161536
  59.7 1.9 copy.49
  61.6 0.0 copy-start.2
  61.6 2.0 concatenate.12.clone
  63.6 0.3 copy-done.2
  63.8 1.5 concatenate.13.clone
  65.3 2.7 %copy.23 = f32[16,256,128]{1,2,0:T(8,128)} copy(bf16[16,256,128]{2,1,0:T(8,128)(2,1)} %all-gather.3.cloned.1.call-done) | data formatting | bytes 3145728 | tf_op jit(solution)/shard_map/convert_element_type | solution.py:8
  68.0 0.0 copy-done
  68.0 5.8 %convert_bitcast_fusion = bf16[5,16,256,128]{2,3,1,0:T(8,128)(2,1)} fusion(f32[16,256,128]{1,2,0:T(8,128)} %concatenate.13.clone, f32[5,128]{1,0:T(8,128)S(1)} %get-tuple-element.15, f32[16,256,128]{1,2,0:T(8,128)S(1)} %concatenate.12.clone, f32[5,128]{1,0:T(8,128)S(1)} %get-tuple-element.16, f32[16,256,128]{1,2,0:T(8,128)} %copy.23, ...), kind=kOutput, calls=%fused_computation.5 | convolution fusion | flops 1360527360 | bytes 12197376 | tf_op jit(solution)/shard_map/tbq,trqj->trbj/dot_general | solution.py:24
  73.8 8.3 %copy.26 = bf16[5,16,256,128]{3,1,0,2:T(8,128)(2,1)} copy(bf16[5,16,256,128]{2,3,1,0:T(8,128)(2,1)} %convert_bitcast_fusion) | data formatting | bytes 10485760 | tf_op jit(solution)/shard_map/convert_element_type | solution.py:26
  82.0 0.0 copy-start.4
  82.0 0.0 copy-start.1
  82.0 10.6 %all-to-all-start = ((bf16[5,16,256,128]{3,1,0,2:T(8,128)(2,1)}), bf16[5,16,256,128]{3,1,0,2:T(8,128)(2,1)}, u32[]{:S(2)}, u32[]{:S(2)}) async-start(bf16[5,16,256,128]{3,1,0,2:T(8,128)(2,1)} %copy.26), calls=%async_computation | async-start | bytes 10485760 | tf_op jit(solution)/shard_map/all_to_all | solution.py:30
  92.7 0.0 all-gather.5.cloned.1.call-start
  92.7 0.0 copy-done.4
  92.7 0.0 copy-done.1
  92.7 0.2 copy.29
  93.0 0.4 fusion.21
  93.4 0.7 copy.50
  94.1 0.6 concatenate.14.clone
  94.7 0.0 copy-start.5
  94.7 0.7 copy.51
  95.4 0.2 concatenate.15.clone
  95.6 0.0 copy-done.5
  95.6 2.8 %fusion.18 = bf16[5,16,4,128]{3,2,1,0:T(4,128)(2,1)} fusion(f32[256,16,128]{2,0,1:T(8,128)S(1)} %concatenate.15.clone, f32[5,128]{1,0:T(8,128)S(1)} %get-tuple-element.17, f32[256,16,128]{2,0,1:T(8,128)S(1)} %concatenate.14.clone, f32[5,128]{1,0:T(8,128)S(1)} %get-tuple-element.18, f32[256,16,128]{2,0,1:T(8,128)S(1)} %copy.29, f32[5,128]{1,0:T(8,128)S(1)} %bitcast.50, ...), kind=kOutput, calls=%fused_computation.18 | convolution fusion | flops 36741120 | bytes 6391296 | tf_op jit(solution)/shard_map/tpq,tqrs->trps/dot_general | solution.py:18
  98.4 0.0 all-gather.5.cloned.1.call-update
  98.4 0.2 reduce-scatter.2.cloned.1.call-start
  98.7 60.2 %all-to-all-done = bf16[5,16,256,128]{3,1,0,2:T(8,128)(2,1)} async-done(((bf16[5,16,256,128]{3,1,0,2:T(8,128)(2,1)}), bf16[5,16,256,128]{3,1,0,2:T(8,128)(2,1)}, u32[]{:S(2)}, u32[]{:S(2)}) %all-to-all-start) | async-done | bytes 5242912 | tf_op jit(solution)/shard_map/all_to_all | solution.py:30
  158.8 6.2 %copy.28 = bf16[5,16,16,16,128]{4,3,2,1,0:T(8,128)(2,1)} copy(bf16[5,16,16,16,128]{4,2,0,3,1:T(8,128)(2,1)} %bitcast.6) | data formatting | bytes 10485760 | tf_op jit(solution)/shard_map/all_to_all | solution.py:30
  165.0 3.6 %all-gather.5.cloned.1.call-done = bf16[5,256,4,128]{3,2,1,0:T(4,128)(2,1)} async-done(((bf16[5,16,4,128]{3,2,1,0:T(4,128)(2,1)}), bf16[5,256,4,128]{3,2,1,0:T(4,128)(2,1)}) %all-gather.5.cloned.1.call-update) | async-done | bytes 1310736 | tf_op jit(solution)/shard_map/all_gather | solution.py:21
  168.7 0.0 copy-start.3
  168.7 7.7 %fusion.12 = bf16[128,4,16,128]{3,0,1,2:T(8,128)(2,1)} fusion(bf16[5,256,16,128,1]{3,2,1,0,4:T(8,128)(2,1)} %bitcast.46, bf16[5,256,4,128]{3,2,1,0:T(4,128)(2,1)} %all-gather.5.cloned.1.call-done), kind=kOutput, calls=%fused_computation.14 | convolution fusion | flops 2685403136 | bytes 8650752 | tf_op jit(solution)/shard_map/trai,trbj->jabi/dot_general | solution.py:27
  176.4 0.0 reduce-scatter.2.cloned.1.call-update
  176.4 48.5 %reduce-scatter.2.cloned.1.call-done = bf16[32,4,16,128]{3,0,1,2:T(8,128)(2,1)} async-done(((bf16[128,4,16,128]{3,0,1,2:T(8,128)(2,1)}), bf16[32,4,16,128]{3,0,1,2:T(8,128)(2,1)}) %reduce-scatter.2.cloned.1.call-update) | async-done | bytes 524304 | tf_op jit(solution)/shard_map/reduce_scatter | solution.py:33
  224.9 0.0 copy-done.3
  224.9 1.4 subtract_convert_fusion
  226.3 1.1 copy.34
  (5 shorter events, 0.0 us)
Async XLA Ops:
  7.4 60.6 %copy-start = (bf16[5,256,256]{2,1,0:T(8,128)(2,1)S(1)}, bf16[5,256,256]{2,1,0:T(8,128)(2,1)}, u32[]{:S(2)}) copy-start(bf16[5,256,256]{2,1,0:T(8,128)(2,1)} %param.10) | copy-start | bytes 1966084
  7.4 46.0 %all-gather.3.cloned.1.call-start = ((), (), s32[]{:S(2)}) async-start(), calls=%async_computation.2 | async-start | bytes 1179648 | tf_op jit(solution)/shard_map/all_gather | solution.py:22
  61.6 2.2 copy-start.2
  82.0 10.7 %copy-start.4 = (f32[5,3,128]{2,1,0:T(4,128)S(1)}, f32[5,3,128]{2,1,0:T(4,128)}, u32[]{:S(2)}) copy-start(f32[5,3,128]{2,1,0:T(4,128)} %param.11) | copy-start | bytes 23044
  82.0 10.7 %copy-start.1 = (bf16[256,16,128]{2,1,0:T(8,128)(2,1)S(1)}, bf16[256,16,128]{2,1,0:T(8,128)(2,1)}, u32[]{:S(2)}) copy-start(bf16[256,16,128]{2,1,0:T(8,128)(2,1)} %param.7) | copy-start | bytes 3145732
  82.0 76.8 %all-to-all-start = ((bf16[5,16,256,128]{3,1,0,2:T(8,128)(2,1)}), bf16[5,16,256,128]{3,1,0,2:T(8,128)(2,1)}, u32[]{:S(2)}, u32[]{:S(2)}) async-start(bf16[5,16,256,128]{3,1,0,2:T(8,128)(2,1)} %copy.26), calls=%async_computation | async-start | bytes 10485760 | tf_op jit(solution)/shard_map/all_to_all | solution.py:30
  92.7 76.0 %all-gather.5.cloned.1.call-start = ((), (), s32[]{:S(2)}) async-start(), calls=%async_computation.3 | async-start | bytes 1392640 | tf_op jit(solution)/shard_map/all_gather | solution.py:21
  94.7 0.9 copy-start.5
  98.4 126.4 %reduce-scatter.2.cloned.1.call-start = ((), (), s32[]{:S(2)}) async-start(), calls=%async_computation.4 | async-start | bytes 2621440 | tf_op jit(solution)/shard_map/reduce_scatter | solution.py:33
  168.7 56.2 %copy-start.3 = (bf16[32,4,16,128]{3,2,1,0:T(8,128)(2,1)S(1)}, bf16[32,4,16,128]{3,2,1,0:T(8,128)(2,1)}, u32[]{:S(2)}) copy-start(bf16[32,4,16,128]{3,2,1,0:T(8,128)(2,1)} %param.13) | copy-start | bytes 1572868
Sparse Core Ops, SparseCore 0:
  10.3 43.0 all-gather.2
  176.5 48.3 reduce-scatter.1
Sparse Core Ops, SparseCore 1:
  98.5 70.1 all-gather.4
where the time goes:
time: 235 us
  waiting for transfers between devices  157 us (67%)
  local copies, waits for them, and re-layouts  33.9 us (14%)
  matrix products  16.2 us (7%)
  between operations  15 us (6%)
  starting transfers between devices  10.9 us (5%)
    all_to_all x1, waiting for transfers between devices, on_device(): lax.all_to_all(right_frame, 'rcol', split_axis=2, concat_axis=1, tiled=True)  60.2 us
    reduce_scatter x1, waiting for transfers between devices, on_device(): lax.psum_scatter(partial_sum.astype(jnp.bfloat16), 'term', scatter_dimens...  48.5 us
    all_gather x1, waiting for transfers between devices, on_device(): right_block = lax.all_gather(core_right, 'lrow', axis=1, tiled=True)  44.4 us
    all_to_all x1, starting transfers between devices, on_device(): lax.all_to_all(right_frame, 'rcol', split_axis=2, concat_axis=1, tiled=True)  10.6 us
    convert_element_type x1, local copies, waits for them, and re-layouts, on_device(): right_frame = jnp.einsum('tbq,trqj->trbj', env_right, right_field, prefer...  8.27 us
    dot_general x1, matrix products, on_device(): jnp.einsum('trai,trbj->jabi', left_frame, lax.all_to_all(right_frame, 'rc...  7.68 us
    unnamed x20, local copies, waits for them, and re-layouts  6.47 us
    all_to_all x1, local copies, waits for them, and re-layouts, on_device(): lax.all_to_all(right_frame, 'rcol', split_axis=2, concat_axis=1, tiled=True)  6.22 us
  transfers between devices with their start and end apart: 4, of which 4 were waited for; matrix products, arithmetic and copies ran while one was open for 5% of the time, Pallas kernels for 0%

commit v1 on v0

v1 whole, which is shorter than its diff:
```python
import jax
import jax.numpy as jnp
from jax import lax
from jax.experimental import pallas as pl
from jax.experimental.pallas import tpu as pltpu
from jax.sharding import Mesh, PartitionSpec as P

BF16, F32 = jnp.bfloat16, jnp.float32
RCOL = ("x1", "x0", "y", "core")


def spread(block, axes, count):
    return lax.all_to_all(
        jnp.broadcast_to(block[None], (count,) + block.shape), axes, 0, 0, tiled=True
    )


def frames_kernel(coef_ref, env_ref, core_ref, left_ref, out_ref, raw, frame):
    terms, points, ranks, rows = 20, 16, 128, 64
    group = 4

    def make(step, carry):
        start = pl.multiple_of(step * group * rows, group * rows)
        raw[...] = lax.dot_general(
            env_ref[pl.ds(start, group * rows), :],
            core_ref[...],
            (((1,), (1,)), ((), ())),
            preferred_element_type=F32,
        )
        for at in range(group):
            t = step * group + at
            top = at * rows
            columns = pl.ds(pl.multiple_of(t * ranks, ranks), ranks)
            for j in range(points):
                value = (
                    coef_ref[t, j] * raw[top : top + rows, (j + 1) * ranks : (j + 2) * ranks]
                    + coef_ref[t, points + j] * raw[top : top + rows, j * ranks : (j + 1) * ranks]
                    + coef_ref[t, 2 * points + j] * raw[top : top + rows, (j + 2) * ranks : (j + 3) * ranks]
                )
                frame[j * rows : (j + 1) * rows, columns] = value.astype(BF16)
        return carry

    lax.fori_loop(0, terms // group, make, 0)

    def contract(step, carry):
        start = pl.multiple_of(step * 4 * rows, 4 * rows)
        part = jnp.dot(frame[pl.ds(start, 4 * rows), :], left_ref[...], preferred_element_type=F32).astype(BF16)
        for at in range(4):
            for dest in range(4):
                for a in range(4):
                    out_ref[dest, step * 4 + at, a] = part[
                        at * rows + dest * 16 : at * rows + dest * 16 + 16, a * 128 : (a + 1) * 128
                    ]
        return carry

    lax.fori_loop(0, points // 4, contract, 0)


def frames_and_product(coef, env, core, left):
    vmem = pl.BlockSpec(memory_space=pltpu.VMEM)
    return pl.pallas_call(
        frames_kernel,
        out_shape=jax.ShapeDtypeStruct((4, 16, 4, 16, 128), BF16),
        in_specs=[pl.BlockSpec(memory_space=pltpu.SMEM), vmem, vmem, vmem],
        out_specs=vmem,
        scratch_shapes=[pltpu.VMEM((256, 18 * 128), F32), pltpu.VMEM((1024, 2560), BF16)],
        compiler_params=pltpu.CompilerParams(vmem_limit_bytes=40 << 20),
        cost_estimate=pl.CostEstimate(flops=4_200_000_000, bytes_accessed=8_000_000, transcendentals=0),
    )(coef, env, core, left)


def on_device(core_left, core_right, env_left, env_right, coef_left, coef_right, projected):
    x0, x1 = lax.axis_index("x0"), lax.axis_index("x1")
    core, term = lax.axis_index("core"), lax.axis_index("term")
    swap = [(0, 1), (1, 0)]

    points = core_right.reshape(512, 128).T
    points = jnp.pad(points, ((1, 1), (0, 0)))
    mine = lax.dynamic_slice(points, (term * 32, 0), (34, 512))
    windows = jnp.stack([mine[:18], mine[16:]]).reshape(1, 2, 72, 128)
    windows = jnp.broadcast_to(windows, (16, 2, 72, 128)).reshape(32, 72, 128)
    slices = lax.all_to_all(windows, ("lrow", "x1", "x0"), 0, 0, tiled=True)
    slices = slices.reshape(8, 4, 18, 16, 32).transpose(2, 1, 3, 0, 4).reshape(18, 64, 256)
    other = lax.ppermute(slices, "core", swap)
    second = jnp.concatenate([slices, other], axis=1).reshape(18 * 128, 256)

    small = jnp.concatenate(
        [
            env_left.astype(F32).reshape(40, 128),
            coef_left.reshape(15, 128),
            coef_right.reshape(15, 128),
            jnp.zeros((2, 128), F32),
        ]
    )
    small = spread(small, "term", 4).reshape(4, 72, 128)
    envs = small[:, :40].reshape(80, 256).astype(BF16)
    lefts = small[:, 40:55].reshape(20, 3, 1, 1, 128)
    rights = small[:, 55:70].reshape(20, 3, 128)

    raw = jnp.dot(envs, core_left.reshape(256, 2048), preferred_element_type=F32).reshape(20, 4, 16, 128)
    before = jnp.pad(raw[..., :-1], ((0, 0), (0, 0), (0, 0), (1, 0)))
    after = jnp.pad(raw[..., 1:], ((0, 0), (0, 0), (0, 0), (0, 1)))
    frame = lefts[:, 0] * raw + lefts[:, 1] * before + lefts[:, 2] * after
    frame = frame.astype(BF16).transpose(0, 2, 1, 3).reshape(20 * 16, 512)
    frame = spread(frame, ("x1", "x0"), 4)
    frame = frame.reshape(4, 20, 16, 512).transpose(1, 0, 2, 3).reshape(20, 64, 512)
    other = lax.ppermute(frame, "core", swap)
    left = jnp.concatenate([frame, other], axis=1).reshape(2560, 512)

    rows = env_right.reshape(5, 2, 4, 2, 16, 256)
    rows = lax.dynamic_slice(rows, (0, x1, 0, core, 0, 0), (5, 1, 4, 1, 16, 256)).reshape(320, 256)
    env = spread(rows, "term", 4).reshape(1280, 256)

    coef = lax.dynamic_slice(rights, (0, 0, term * 32 + x0 * 16), (20, 3, 16)).reshape(20, 48)
    part = frames_and_product(coef, env, second, left)
    part = lax.all_to_all(part, ("x0", "y"), 0, 0, tiled=True).reshape(2, 2, 16, 4, 16, 128)
    summed = (part[:, 0].astype(F32) + part[:, 1].astype(F32)).reshape(32, 4, 16, 128)
    return (projected.astype(F32) - summed).astype(BF16)


def solution(mesh):
    split = Mesh(mesh.devices.reshape(8, 2, 2, 2, 2, 4), ("lrow",) + RCOL + ("term",))
    return jax.shard_map(
        on_device,
        mesh=split,
        in_specs=(
            P(None, RCOL, None),
            P(RCOL, "lrow", None),
            P("term", "lrow", None),
            P("term", None, None),
            P("term", None, None),
            P("term", None, None),
            P("term", "lrow", RCOL, None),
        ),
        out_specs=P("term", "lrow", RCOL, None),
        check_vma=False,
    )
```

time: 235 us -> 123 us (0.52)
  waiting for transfers between devices: 157 us -> 28.5 us
  starting transfers between devices: 10.9 us -> 41.1 us
  blocking collectives: 0 us -> 16.1 us
  matrix products: 16.2 us -> 0.45 us
  between operations: 15 us -> 0.27 us
  local copies, waits for them, and re-layouts: 33.9 us -> 22.1 us
  Pallas kernels: 0 us -> 8.22 us
  other arithmetic: 1.41 us -> 4.57 us
    reduce_scatter x1 -> x0, waiting for transfers between devices: 48.5 us -> none  [on_device(): lax.psum_scatter(partial_sum.astype(jnp.bfloat16), 'term', scatter_dimens...]
    all_gather x2 -> x0, waiting for transfers between devices: 48.1 us -> none  [the longest x1 44.4 us: on_device(): right_block = lax.all_gather(core_right, 'lrow', axis=1, tiled=True)]
    all_to_all x1 -> x4, waiting for transfers between devices: 60.2 us -> 27.2 us  [the longest x3 20.4 us: spread(): lax.all_to_all(jnp.broadcast_to(block[None], (count,) + block.shape), axe...]
    all_to_all x1 -> x4, starting transfers between devices: 10.6 us -> 28 us  [the longest x3 17 us: spread(): lax.all_to_all(jnp.broadcast_to(block[None], (count,) + block.shape), axe...]
    all_to_all x0 -> x1, blocking collectives: none -> 16.1 us  [on_device(): lax.all_to_all(part, ('x0', 'y'), 0, 0, tiled=True)]
    dot_general x3 -> x1, matrix products: 16.2 us -> 0.45 us  [on_device(): jnp.dot(envs, core_left.reshape(256, 2048), preferred_element_type=F32)]
    ppermute x0 -> x2, starting transfers between devices: none -> 13.1 us  [the longest x1 7.14 us: on_device(): other = lax.ppermute(slices, 'core', swap)]
    convert_element_type x4 -> x1, local copies, waits for them, and re-layouts: 12.3 us -> 0.03 us  [on_device(): envs = small[:, :40].reshape(80, 256).astype(BF16)]
  transfers between devices with their start and end apart: 4 -> 6, of which waited for: 4 -> 4; matrix products, arithmetic and copies ran while one was open for 5% -> 15% of each run, Pallas kernels for 0% -> 0%
where the time goes in v1:
time: 123 us; the launch traced here: 121 us
  starting transfers between devices  41.1 us (33%)
  waiting for transfers between devices  28.5 us (23%)
  local copies, waits for them, and re-layouts  22.1 us (18%)
  blocking collectives  16.1 us (13%)
  Pallas kernels  8.22 us (7%)
  other arithmetic  4.57 us (4%)
    all_to_all x3, waiting for transfers between devices, spread(): lax.all_to_all(jnp.broadcast_to(block[None], (count,) + block.shape), axe...  20.4 us
    all_to_all x3, starting transfers between devices, spread(): lax.all_to_all(jnp.broadcast_to(block[None], (count,) + block.shape), axe...  17 us
    all_to_all x1, blocking collectives, on_device(): lax.all_to_all(part, ('x0', 'y'), 0, 0, tiled=True)  16.1 us
    all_to_all x1, starting transfers between devices, on_device(): slices = lax.all_to_all(windows, ('lrow', 'x1', 'x0'), 0, 0, tiled=True)  11.1 us
    pallas_call x1, Pallas kernels, frames_and_product(): pl.pallas_call(frames_kernel, out_shape=jax.ShapeDtypeStruct((4, 16, 4, 1...  8.22 us
    ppermute x1, starting transfers between devices, on_device(): other = lax.ppermute(slices, 'core', swap)  7.14 us
    all_to_all x1, waiting for transfers between devices, on_device(): slices = lax.all_to_all(windows, ('lrow', 'x1', 'x0'), 0, 0, tiled=True)  6.73 us
    reshape x2, local copies, waits for them, and re-layouts, on_device(): slices.reshape(8, 4, 18, 16, 32).transpose(2, 1, 3, 0, 4)  6.2 us
  transfers between devices with their start and end apart: 6, of which 4 were waited for; matrix products, arithmetic and copies ran while one was open for 15% of the time, Pallas kernels for 0%

profile of v1, /device:TPU:1, one launch (start us, length us, event | category | flops | bytes accessed | tf_op | source)
XLA Modules:
  0.0 121.3 jit_solution(13676796603820314510)
XLA Ops:
  0.0 0.0 copy-start
  0.0 0.8 reshape.100
  0.8 0.7 reshape.82
  1.5 0.7 reshape.83
  2.2 0.1 pad.24.clone
  2.3 0.1 maximum_maximum_fusion
  2.4 0.7 broadcast_in_dim.31
  3.0 7.6 %all-to-all-start = ((f32[4,72,128]{2,1,0:T(8,128)}), f32[4,72,128]{2,1,0:T(8,128)S(1)}, u32[]{:S(2)}, u32[]{:S(2)}) async-start(f32[4,72,128]{2,1,0:T(8,128)} %broadcast_in_dim.31), calls=%async_computation | async-start | bytes 294912 | tf_op jit(solution)/shard_map/all_to_all | solution.py:13
  10.7 1.5 %copy.38 = bf16[32,8,16,128]{3,1,2,0:T(8,128)(2,1)S(1)} copy(bf16[32,8,16,128]{3,2,1,0:T(8,128)(2,1)} %bitcast.59) | data formatting | bytes 2097152
  12.2 0.5 copy.18
  12.7 5.6 %all-to-all-done = f32[4,72,128]{2,1,0:T(8,128)S(1)} async-done(((f32[4,72,128]{2,1,0:T(8,128)}), f32[4,72,128]{2,1,0:T(8,128)S(1)}, u32[]{:S(2)}, u32[]{:S(2)}) %all-to-all-start) | async-done | bytes 147488 | tf_op jit(solution)/shard_map/all_to_all | solution.py:13
  18.5 0.5 fusion.2
  18.9 0.3 fusion.4
  19.2 0.3 fusion.1
  19.5 0.3 copy.20
  19.8 0.0 copy-start.4
  19.9 1.2 broadcast_in_dim.37
  21.0 4.0 %all-to-all-start.3 = ((bf16[4,320,512]{2,1,0:T(8,128)(2,1)}), bf16[4,320,512]{2,1,0:T(8,128)(2,1)S(1)}, u32[]{:S(2)}, u32[]{:S(2)}) async-start(bf16[4,320,512]{2,1,0:T(8,128)(2,1)} %broadcast_in_dim.37), calls=%async_computation.3 | async-start | bytes 2621440 | tf_op jit(solution)/shard_map/all_to_all | solution.py:13
  25.0 0.0 copy-done.4
  25.0 0.1 copy.16
  25.3 14.8 %all-to-all-done.3 = bf16[4,320,512]{2,1,0:T(8,128)(2,1)S(1)} async-done(((bf16[4,320,512]{2,1,0:T(8,128)(2,1)}), bf16[4,320,512]{2,1,0:T(8,128)(2,1)S(1)}, u32[]{:S(2)}, u32[]{:S(2)}) %all-to-all-start.3) | async-done | bytes 1310752 | tf_op jit(solution)/shard_map/all_to_all | solution.py:13
  40.1 0.9 broadcast_in_dim.35
  41.0 11.1 %all-to-all-start.2 = ((bf16[32,72,128]{2,1,0:T(8,128)(2,1)}), bf16[32,72,128]{2,1,0:T(8,128)(2,1)S(1)}, u32[]{:S(2)}, u32[]{:S(2)}) async-start(bf16[32,72,128]{2,1,0:T(8,128)(2,1)} %bitcast.7), calls=%async_computation.2 | async-start | bytes 1179648 | tf_op jit(solution)/shard_map/all_to_all | solution.py:82
  52.1 1.2 copy.21
  53.2 5.9 %collective-permute-start.1 = (bf16[20,64,512]{2,1,0:T(8,128)(2,1)}, bf16[20,64,512]{2,1,0:T(8,128)(2,1)}, u32[]{:S(2)}, u32[]{:S(2)}) collective-permute-start(bf16[20,64,512]{2,1,0:T(8,128)(2,1)} %bitcast.17), channel_id=1, source_target_pairs={{0,4},{4,0},{1,5},{5,1},{2,6},{6,2},{3,7},{7,3},{8,12},{12,8},{9,1... | collective-permute-start | bytes 3932168 | tf_op jit(solution)/shard_map/ppermute | solution.py:107
  59.2 6.7 %all-to-all-done.2 = bf16[32,72,128]{2,1,0:T(8,128)(2,1)S(1)} async-done(((bf16[32,72,128]{2,1,0:T(8,128)(2,1)}), bf16[32,72,128]{2,1,0:T(8,128)(2,1)S(1)}, u32[]{:S(2)}, u32[]{:S(2)}) %all-to-all-start.2) | async-done | bytes 589856 | tf_op jit(solution)/shard_map/all_to_all | solution.py:82
  66.0 1.0 broadcast_in_dim.33
  66.9 0.1 copy-done.2
  67.0 5.3 %all-to-all-start.1 = ((bf16[4,320,256]{2,1,0:T(8,128)(2,1)}), bf16[4,320,256]{2,1,0:T(8,128)(2,1)}, u32[]{:S(2)}, u32[]{:S(2)}) async-start(bf16[4,320,256]{2,1,0:T(8,128)(2,1)} %broadcast_in_dim.33), calls=%async_computation.1 | async-start | bytes 1310720 | tf_op jit(solution)/shard_map/all_to_all | solution.py:13
  72.4 2.8 %reshape.90 = bf16[8,4,18,16,32]{4,3,2,1,0:T(8,128)(2,1)S(1)} reshape(bf16[32,72,128]{2,1,0:T(8,128)(2,1)} %copy-done.2) | data formatting | bytes 1179648 | tf_op jit(solution)/shard_map/reshape | solution.py:83
  75.2 4.2 %copy.17 = bf16[18,4,16,8,32]{4,3,2,1,0:T(8,128)(2,1)} copy(bf16[18,4,16,8,32]{4,2,0,1,3:T(8,128)(2,1)S(1)} %bitcast.52) | data formatting | bytes 1179648 | tf_op jit(solution)/shard_map/transpose | solution.py:83
  79.3 3.4 %reshape.91 = bf16[18,64,256]{2,1,0:T(8,128)(2,1)S(1)} reshape(bf16[18,4,16,8,32]{4,3,2,1,0:T(8,128)(2,1)} %copy.17) | data formatting | bytes 1179648 | tf_op jit(solution)/shard_map/reshape | solution.py:83
  82.7 7.1 %collective-permute-start = (bf16[18,64,256]{2,1,0:T(8,128)(2,1)S(1)}, bf16[18,64,256]{2,1,0:T(8,128)(2,1)S(1)}, u32[]{:S(2)}, u32[]{:S(2)}) collective-permute-start(bf16[18,64,256]{2,1,0:T(8,128)(2,1)S(1)} %reshape.91), channel_id=1, source_target_pairs={{0,4},{4,0},{1,5},{5,1},{2,6},{6,2},{3,7},{7,3},{8,12},{12,8},{9,1... | collective-permute-start | bytes 1769480 | tf_op jit(solution)/shard_map/ppermute | solution.py:84
  89.9 0.1 constant_dynamic-slice_fusion.1
  90.0 0.1 copy.15
  90.1 0.1 copy.22.coef_ref
  90.2 1.3 %collective-permute-done = bf16[18,64,256]{2,1,0:T(8,128)(2,1)S(1)} collective-permute-done((bf16[18,64,256]{2,1,0:T(8,128)(2,1)S(1)}, bf16[18,64,256]{2,1,0:T(8,128)(2,1)S(1)}, u32[]{:S(2)}, u32[]{:S(2)}) %collective-permute-start) | collective-permute-done | bytes 589856 | tf_op jit(solution)/shard_map/ppermute | solution.py:84
  91.5 1.2 pad_maximum_fusion.1
  92.6 0.0 collective-permute-done.1
  92.6 1.9 %pad_maximum_fusion = bf16[20,128,512]{2,1,0:T(8,128)(2,1)S(1)} fusion(bf16[20,64,512]{2,1,0:T(8,128)(2,1)} %collective-permute-done.1, bf16[20,64,512]{2,1,0:T(8,128)(2,1)} %bitcast.17), kind=kLoop, calls=%fused_computation | loop fusion | flops 5242880 | bytes 5242880 | tf_op jit(solution)/shard_map/concatenate | solution.py:108
  94.5 0.0 all-to-all-done.1
  94.6 1.3 %copy-done.1 = bf16[18,128,256]{2,1,0:T(8,128)(2,1)S(1)} copy-done((bf16[18,128,256]{2,1,0:T(8,128)(2,1)S(1)}, bf16[18,128,256]{2,1,0:T(8,128)(2,1)}, u32[]{:S(2)}) %copy-start.1) | copy-done | bytes 1179672
  95.8 8.2 %shard_map.73 = bf16[4,16,4,16,128]{4,3,2,1,0:T(8,128)(2,1)S(1)} custom-call(f32[20,48]{1,0:T(8,128)S(1)} %copy.22.coef_ref, bf16[1280,256]{1,0:T(8,128)(2,1)} %bitcast.3.env_ref, bf16[2304,256]{1,0:T(8,128)(2,1)S(1)} %bitcast.51, bf16[2560,512]{1,0:T(8,128)(2,1)S(1)} %bitcast.50), custom_call_target="tpu_custom_call" | custom-call | flops 4200000000 | bytes 8000000 | tf_op jit(solution)/shard_map/pallas_call | solution.py:61
  104.0 0.0 copy-start.3
  104.1 16.1 %all_to_all.25 = bf16[4,16,4,16,128]{4,3,2,1,0:T(8,128)(2,1)S(1)} all-to-all(bf16[4,16,4,16,128]{4,3,2,1,0:T(8,128)(2,1)S(1)} %shard_map.73), channel_id=1, replica_groups=mesh['lrow'=8,'x1'=2,'x0'=2,'y'=2,'core'=2,'term'=4] {'x0','y'}, dimensions={0} | all-to-all | bytes 2097152 | tf_op jit(solution)/shard_map/all_to_all | solution.py:116
  120.2 0.2 convert_add_fusion
  120.3 0.0 copy-done.3
  120.4 1.0 fusion
  (18 shorter events, 0.3 us)
Async XLA Ops:
  0.0 59.2 %copy-start = (bf16[5,256,256]{2,1,0:T(8,128)(2,1)S(1)}, bf16[5,256,256]{2,1,0:T(8,128)(2,1)}, u32[]{:S(2)}) copy-start(bf16[5,256,256]{2,1,0:T(8,128)(2,1)} %param.10) | copy-start | bytes 1966084
  3.0 15.3 %all-to-all-start = ((f32[4,72,128]{2,1,0:T(8,128)}), f32[4,72,128]{2,1,0:T(8,128)S(1)}, u32[]{:S(2)}, u32[]{:S(2)}) async-start(f32[4,72,128]{2,1,0:T(8,128)} %broadcast_in_dim.31), calls=%async_computation | async-start | bytes 294912 | tf_op jit(solution)/shard_map/all_to_all | solution.py:13
  19.8 5.2 %copy-start.4 = (bf16[16,32,128]{2,1,0:T(8,128)(2,1)S(1)}, bf16[16,32,128]{2,1,0:T(8,128)(2,1)}, u32[]{:S(2)}) copy-start(bf16[16,32,128]{2,1,0:T(8,128)(2,1)} %param.8) | copy-start | bytes 393220
  21.0 19.0 %all-to-all-start.3 = ((bf16[4,320,512]{2,1,0:T(8,128)(2,1)}), bf16[4,320,512]{2,1,0:T(8,128)(2,1)S(1)}, u32[]{:S(2)}, u32[]{:S(2)}) async-start(bf16[4,320,512]{2,1,0:T(8,128)(2,1)} %broadcast_in_dim.37), calls=%async_computation.3 | async-start | bytes 2621440 | tf_op jit(solution)/shard_map/all_to_all | solution.py:13
  41.0 25.0 %all-to-all-start.2 = ((bf16[32,72,128]{2,1,0:T(8,128)(2,1)}), bf16[32,72,128]{2,1,0:T(8,128)(2,1)S(1)}, u32[]{:S(2)}, u32[]{:S(2)}) async-start(bf16[32,72,128]{2,1,0:T(8,128)(2,1)} %bitcast.7), calls=%async_computation.2 | async-start | bytes 1179648 | tf_op jit(solution)/shard_map/all_to_all | solution.py:82
  53.2 39.4 %collective-permute-start.1 = (bf16[20,64,512]{2,1,0:T(8,128)(2,1)}, bf16[20,64,512]{2,1,0:T(8,128)(2,1)}, u32[]{:S(2)}, u32[]{:S(2)}) collective-permute-start(bf16[20,64,512]{2,1,0:T(8,128)(2,1)} %bitcast.17), channel_id=1, source_target_pairs={{0,4},{4,0},{1,5},{5,1},{2,6},{6,2},{3,7},{7,3},{8,12},{12,8},{9,1... | collective-permute-start | bytes 3932168 | tf_op jit(solution)/shard_map/ppermute | solution.py:107
  66.0 1.1 copy-start.2
  67.0 27.5 %all-to-all-start.1 = ((bf16[4,320,256]{2,1,0:T(8,128)(2,1)}), bf16[4,320,256]{2,1,0:T(8,128)(2,1)}, u32[]{:S(2)}, u32[]{:S(2)}) async-start(bf16[4,320,256]{2,1,0:T(8,128)(2,1)} %broadcast_in_dim.33), calls=%async_computation.1 | async-start | bytes 1310720 | tf_op jit(solution)/shard_map/all_to_all | solution.py:13
  82.7 8.8 %collective-permute-start = (bf16[18,64,256]{2,1,0:T(8,128)(2,1)S(1)}, bf16[18,64,256]{2,1,0:T(8,128)(2,1)S(1)}, u32[]{:S(2)}, u32[]{:S(2)}) collective-permute-start(bf16[18,64,256]{2,1,0:T(8,128)(2,1)S(1)} %reshape.91), channel_id=1, source_target_pairs={{0,4},{4,0},{1,5},{5,1},{2,6},{6,2},{3,7},{7,3},{8,12},{12,8},{9,1... | collective-permute-start | bytes 1769480 | tf_op jit(solution)/shard_map/ppermute | solution.py:84
  94.5 1.3 %copy-start.1 = (bf16[18,128,256]{2,1,0:T(8,128)(2,1)S(1)}, bf16[18,128,256]{2,1,0:T(8,128)(2,1)}, u32[]{:S(2)}) copy-start(bf16[18,128,256]{2,1,0:T(8,128)(2,1)} %pad_maximum_fusion.1) | copy-start | bytes 3538948
  104.0 16.3 %copy-start.3 = (bf16[32,4,16,128]{3,2,1,0:T(8,128)(2,1)S(1)}, bf16[32,4,16,128]{3,2,1,0:T(8,128)(2,1)}, u32[]{:S(2)}) copy-start(bf16[32,4,16,128]{3,2,1,0:T(8,128)(2,1)} %param.13) | copy-start | bytes 1572868

commit v2 on v1

v2 whole, which is shorter than its diff:
```python
import jax
import jax.numpy as jnp
from jax import lax
from jax.experimental import pallas as pl
from jax.experimental.pallas import tpu as pltpu
from jax.sharding import Mesh, PartitionSpec as P

BF16, F32 = jnp.bfloat16, jnp.float32
RCOL = ("x1", "x0", "y", "core")
VMEM = pl.BlockSpec(memory_space=pltpu.VMEM)
SMEM = pl.BlockSpec(memory_space=pltpu.SMEM)


def shifted(block, axes):
    return [lax.ppermute(block, axes, [(i, (i + shift) % 4) for i in range(4)]) for shift in range(1, 4)]


def unscramble(at, ref, core):
    lane = lax.broadcasted_iota(jnp.int32, (80, 128), 1)
    low, even = lane < 64, (lane // 32) % 2 == 0
    for x in range(4):
        for half in range(2):
            t0, t1, t2, t3 = (
                ref[((half * 4 + m) * 4 + x) * 5 : ((half * 4 + m) * 4 + x + 1) * 5].reshape(80, 128).astype(F32)
                for m in range(4)
            )
            t0, t2 = jnp.where(low, t0, pltpu.roll(t2, 64, 1)), jnp.where(low, pltpu.roll(t0, 64, 1), t2)
            t1, t3 = jnp.where(low, t1, pltpu.roll(t3, 64, 1)), jnp.where(low, pltpu.roll(t1, 64, 1), t3)
            t0, t1 = jnp.where(even, t0, pltpu.roll(t1, 32, 1)), jnp.where(even, pltpu.roll(t0, 96, 1), t1)
            t2, t3 = jnp.where(even, t2, pltpu.roll(t3, 32, 1)), jnp.where(even, pltpu.roll(t2, 96, 1), t3)
            for g, tile in enumerate((t0, t1, t2, t3)):
                tile = tile.astype(BF16)
                for jj in range(5):
                    j = jj * 4 + g
                    if j < 18:
                        top = j * 128 + at * 64 + x * 16
                        core[top : top + 16, half * 128 : half * 128 + 128] = tile[jj * 16 : jj * 16 + 16]


def main_kernel(place_ref, coef_ref, env_hbm, mine_hbm, other_hbm, l0, l1, l2, l3, m0,
                out_ref, env_ref, mine_ref, other_ref, left_ref, frame, core, raw, sem):
    points, ranks, rows, group = 16, 128, 64, 4
    own, column, term = place_ref[0] * 16, place_ref[1], place_ref[2]

    copies = [
        pltpu.make_async_copy(mine_hbm, mine_ref, sem.at[0]),
        pltpu.make_async_copy(other_hbm.at[pl.ds(0, 160)], other_ref, sem.at[1]),
    ]
    for dest in range(4):
        start = pl.multiple_of(dest * 32 + own, 16)
        copies.append(pltpu.make_async_copy(env_hbm.at[:, pl.ds(start, 16), :], env_ref.at[:, dest], sem.at[2 + dest]))
    pieces = []
    for shift, ref in enumerate((l0, l1, l2, l3)):
        top = pl.multiple_of(lax.rem(column - shift + 4, 4) * 16, 16)
        for a in range(4):
            lanes = pl.ds(a * 128, 128)
            twin = m0.at[a] if shift == 0 else other_hbm.at[pl.ds(160 + (shift - 1) * 80 + a * 20, 20)]
            at = 6 + (shift * 4 + a) * 2
            pieces.append(pltpu.make_async_copy(ref.at[a], left_ref.at[:, pl.ds(top, 16), lanes], sem.at[at]))
            pieces.append(pltpu.make_async_copy(twin, left_ref.at[:, pl.ds(top + 64, 16), lanes], sem.at[at + 1]))
    for copy in copies + pieces:
        copy.start()
    copies[0].wait()
    unscramble(0, mine_ref, core)
    copies[1].wait()
    unscramble(1, other_ref, core)
    for copy in copies[2:]:
        copy.wait()

    def make(step, carry):
        parts = []
        for at in range(group):
            t = step * group + at
            t = lax.rem(term - t // 5 + 4, 4) * 5 + lax.rem(t, 5)
            parts.append(env_ref[t].reshape(rows, 256))
        raw[...] = lax.dot_general(
            jnp.concatenate(parts, axis=0), core[...], (((1,), (1,)), ((), ())), preferred_element_type=F32
        )
        for at in range(group):
            t = step * group + at
            rows_at = slice(at * rows, (at + 1) * rows)
            columns = pl.ds(pl.multiple_of(t * ranks, ranks), ranks)
            for j in range(points):
                frame[j * rows : (j + 1) * rows, columns] = (
                    coef_ref[t, j] * raw[rows_at, (j + 1) * ranks : (j + 2) * ranks]
                    + coef_ref[t, points + j] * raw[rows_at, j * ranks : (j + 1) * ranks]
                    + coef_ref[t, 2 * points + j] * raw[rows_at, (j + 2) * ranks : (j + 3) * ranks]
                ).astype(BF16)
        return carry

    lax.fori_loop(0, 5, make, 0)
    for copy in pieces:
        copy.wait()

    def contract(step, carry):
        start = pl.multiple_of(step * 4 * rows, 4 * rows)
        part = jnp.dot(
            frame[pl.ds(start, 4 * rows), :], left_ref[...].reshape(2560, 512), preferred_element_type=F32
        ).astype(BF16)
        for at in range(4):
            for dest in range(4):
                top = at * rows + dest * 16
                for a in range(4):
                    out_ref[dest, step * 4 + at, a] = part[top : top + 16, a * 128 : (a + 1) * 128]
        return carry

    lax.fori_loop(0, points // 4, contract, 0)


def main_product(place, coef, env, mine, other, pieces):
    anywhere = pl.BlockSpec(memory_space=pl.ANY)
    return pl.pallas_call(
        main_kernel,
        out_shape=jax.ShapeDtypeStruct((4, 16, 4, 16, 128), BF16),
        in_specs=[SMEM, SMEM] + [anywhere] * 8,
        out_specs=VMEM,
        scratch_shapes=[
            pltpu.VMEM((20, 4, 16, 256), BF16),
            pltpu.VMEM((160, 16, 128), BF16),
            pltpu.VMEM((160, 16, 128), BF16),
            pltpu.VMEM((20, 128, 512), BF16),
            pltpu.VMEM((1024, 2560), BF16),
            pltpu.VMEM((18 * 128, 256), BF16),
            pltpu.VMEM((256, 18 * 128), F32),
            pltpu.SemaphoreType.DMA((38,)),
        ],
        compiler_params=pltpu.CompilerParams(vmem_limit_bytes=24 << 20),
        cost_estimate=pl.CostEstimate(flops=4_200_000_000, bytes_accessed=8_000_000, transcendentals=0),
    )(place, coef, env, mine, other, *pieces)


def on_device(core_left, core_right, env_left, env_right, coef_left, coef_right, projected):
    x0, x1 = lax.axis_index("x0"), lax.axis_index("x1")
    core, term = lax.axis_index("core"), lax.axis_index("term")
    swap = [(0, 1), (1, 0)]

    env = lax.dynamic_slice(env_right, (0, x1 * 128, 0), (5, 128, 256))
    env, core_right = lax.optimization_barrier((env, core_right))
    env = lax.all_gather(env, "term", axis=0, tiled=True)

    points = core_right.reshape(512, 128).T
    points = jnp.pad(points, ((1, 3), (0, 0)))
    mine = lax.dynamic_slice(points, (term * 32, 0), (36, 512))
    windows = jnp.stack([mine[:20], mine[16:]]).reshape(2, 5, 4, 16, 32).transpose(0, 1, 3, 2, 4)
    windows = jnp.broadcast_to(windows.reshape(1, 2, 80, 128), (16, 2, 80, 128)).reshape(32, 80, 128)
    windows, env_left = lax.optimization_barrier((windows, env_left))
    slices = lax.all_to_all(windows, ("lrow", "x1", "x0"), 0, 0, tiled=True).reshape(2560, 128)

    zero = jnp.zeros((5, 1, 128), F32)
    wide = env_left.astype(F32)
    small = jnp.concatenate([wide[..., :128], wide[..., 128:], coef_left, zero, coef_right, zero], axis=1)
    small = jnp.concatenate([small] + shifted(small, "term"))
    envs = jnp.concatenate([small[:, :4], small[:, 4:8]], axis=-1).transpose(1, 0, 2).reshape(80, 256).astype(BF16)
    lefts = small[:, 8:11].reshape(1, 20, 3, 1, 128)
    rights = small[:, 12:15]

    raw = jnp.dot(envs, core_left.reshape(256, 2048), preferred_element_type=F32).reshape(4, 20, 16, 128)
    before = jnp.pad(raw[..., :-1], ((0, 0), (0, 0), (0, 0), (1, 0)))
    after = jnp.pad(raw[..., 1:], ((0, 0), (0, 0), (0, 0), (0, 1)))
    left = lefts[:, :, 0] * raw + lefts[:, :, 1] * before + lefts[:, :, 2] * after
    left = left.astype(BF16).reshape(1280, 128)
    others = shifted(left, ("x1", "x0"))
    twin = lax.ppermute(left, "core", swap)
    slices, env, twin, *others = lax.optimization_barrier((slices, env, twin, *others))
    exchanged = lax.ppermute(jnp.concatenate([slices] + others), "core", swap)

    place = jnp.stack([core, x1 * 2 + x0, term])
    coef = lax.dynamic_slice(rights, (0, 0, term * 32 + x0 * 16), (20, 3, 16)).reshape(20, 48)
    pieces = [piece.reshape(4, 20, 16, 128) for piece in [left] + others + [twin]]
    part = main_product(
        place, coef, env, slices.reshape(160, 16, 128), exchanged.reshape(400, 16, 128), pieces
    )
    part = lax.all_to_all(part, ("x0", "y"), 0, 0, tiled=True).reshape(2, 2, 16, 4, 16, 128)
    summed = (part[:, 0].astype(F32) + part[:, 1].astype(F32)).reshape(32, 4, 16, 128)
    return (projected.astype(F32) - summed).astype(BF16)


def solution(mesh):
    split = Mesh(mesh.devices.reshape(8, 2, 2, 2, 2, 4), ("lrow",) + RCOL + ("term",))
    return jax.shard_map(
        on_device,
        mesh=split,
        in_specs=(
            P(None, RCOL, None),
            P(RCOL, "lrow", None),
            P("term", "lrow", None),
            P("term", None, None),
            P("term", None, None),
            P("term", None, None),
            P("term", "lrow", RCOL, None),
        ),
        out_specs=P("term", "lrow", RCOL, None),
        check_vma=False,
    )
```

time: 123 us -> 113 us (0.919)
  local copies, waits for them, and re-layouts: 22.1 us -> 7.02 us
  between operations: 0.27 us -> 13.7 us
  waiting for transfers between devices: 28.5 us -> 16.5 us
  starting transfers between devices: 41.1 us -> 44 us
  Pallas kernels: 8.22 us -> 10.5 us
    all_to_all x4 -> x1, waiting for transfers between devices: 27.2 us -> 0.01 us  [on_device(): lax.all_to_all(windows, ('lrow', 'x1', 'x0'), 0, 0, tiled=True)]
    ppermute x2 -> x8, starting transfers between devices: 13.1 us -> 31.1 us  [the longest x6 23.8 us: shifted(): lax.ppermute(block, axes, [(i, (i + shift) % 4) for i in range(4)])]
    ppermute x2 -> x8, waiting for transfers between devices: 1.32 us -> 16.4 us  [the longest x6 13.3 us: shifted(): lax.ppermute(block, axes, [(i, (i + shift) % 4) for i in range(4)])]
    all_to_all x4 -> x1, starting transfers between devices: 28 us -> 12.9 us  [on_device(): lax.all_to_all(windows, ('lrow', 'x1', 'x0'), 0, 0, tiled=True)]
    reshape x7 -> x1, local copies, waits for them, and re-layouts: 8.42 us -> 0.01 us  [on_device(): lefts = small[:, 8:11].reshape(1, 20, 3, 1, 128)]
    transpose x3 -> x1, local copies, waits for them, and re-layouts: 5.61 us -> 0.07 us  [on_device(): jnp.stack([mine[:20], mine[16:]]).reshape(2, 5, 4, 16, 32)]
    broadcast_in_dim x5 -> x2, local copies, waits for them, and re-layouts: 3.72 us -> 1.08 us  [on_device(): jnp.broadcast_to(windows.reshape(1, 2, 80, 128), (16, 2, 80, 128))]
    pallas_call x1, Pallas kernels: 8.22 us -> 10.5 us  [main_product(): pl.pallas_call(main_kernel, out_shape=jax.ShapeDtypeStruct((4, 16, 4, 16,...]
  transfers between devices with their start and end apart: 6 -> 10, of which waited for: 4 -> 4; matrix products, arithmetic and copies ran while one was open for 15% -> 5% of each run, Pallas kernels for 0% -> 0%
where the time goes in v2:
time: 113 us; the launch traced here: 112 us
  starting transfers between devices  44 us (39%)
  waiting for transfers between devices  16.5 us (15%)
  blocking collectives  16.1 us (14%)
  between operations  13.7 us (12%)
  Pallas kernels  10.5 us (9%)
  local copies, waits for them, and re-layouts  7.02 us (6%)
  other arithmetic  3.74 us (3%)
    ppermute x6, starting transfers between devices, shifted(): lax.ppermute(block, axes, [(i, (i + shift) % 4) for i in range(4)])  23.8 us
    all_to_all x1, blocking collectives, on_device(): lax.all_to_all(part, ('x0', 'y'), 0, 0, tiled=True)  16.1 us
    ppermute x6, waiting for transfers between devices, shifted(): lax.ppermute(block, axes, [(i, (i + shift) % 4) for i in range(4)])  13.3 us
    all_to_all x1, starting transfers between devices, on_device(): lax.all_to_all(windows, ('lrow', 'x1', 'x0'), 0, 0, tiled=True)  12.9 us
    pallas_call x1, Pallas kernels, main_product(): pl.pallas_call(main_kernel, out_shape=jax.ShapeDtypeStruct((4, 16, 4, 16,...  10.5 us
    ppermute x1, starting transfers between devices, on_device(): twin = lax.ppermute(left, 'core', swap)  4.82 us
    ppermute x1, waiting for transfers between devices, on_device(): exchanged = lax.ppermute(jnp.concatenate([slices] + others), 'core', swap)  3.11 us
    unnamed x20, local copies, waits for them, and re-layouts  2.71 us
  transfers between devices with their start and end apart: 10, of which 4 were waited for; matrix products, arithmetic and copies ran while one was open for 5% of the time, Pallas kernels for 0%

profile of v2, /device:TPU:1, one launch (start us, length us, event | category | flops | bytes accessed | tf_op | source)
XLA Modules:
  0.0 112.0 jit_solution(12260923086475025932)
XLA Ops:
  6.5 1.1 copy-done
  7.6 0.7 constant_dynamic-slice_fusion.1
  8.4 0.0 all-gather.2.cloned.1.call-update
  8.4 1.0 copy.27
  9.5 0.0 copy-start.2
  9.5 0.1 stack.25
  9.6 0.1 stack.26
  9.8 0.1 copy.28
  9.8 0.1 broadcast_in_dim.10
  10.0 0.9 broadcast_in_dim.11
  11.0 6.7 %collective-permute-start.2 = (f32[5,16,128]{2,0,1:T(8,128)S(1)}, f32[5,16,128]{2,0,1:T(8,128)S(1)}, u32[]{:S(2)}, u32[]{:S(2)}) collective-permute-start(f32[5,16,128]{2,0,1:T(8,128)S(1)} %constant_dynamic-update-slice_fusion), channel_id=1, source_target_pairs={{0,3},{1,0},{2,1},{3,2},{4,7},{5,4},{6,5},{7,6},{8,11},{9,8},{10,9... | collective-permute-start | bytes 122888 | tf_op jit(solution)/shard_map/ppermute | solution.py:15
  17.7 3.5 %collective-permute-start.1 = (f32[5,16,128]{2,0,1:T(8,128)S(1)}, f32[5,16,128]{2,0,1:T(8,128)}, u32[]{:S(2)}, u32[]{:S(2)}) collective-permute-start(f32[5,16,128]{2,0,1:T(8,128)S(1)} %constant_dynamic-update-slice_fusion), channel_id=1, source_target_pairs={{0,2},{1,3},{2,0},{3,1},{4,6},{5,7},{6,4},{7,5},{8,10},{9,11},{10,... | collective-permute-start | bytes 122888 | tf_op jit(solution)/shard_map/ppermute | solution.py:15
  21.3 4.2 %collective-permute-start = (f32[5,16,128]{2,0,1:T(8,128)S(1)}, f32[5,16,128]{2,0,1:T(8,128)}, u32[]{:S(2)}, u32[]{:S(2)}) collective-permute-start(f32[5,16,128]{2,0,1:T(8,128)S(1)} %constant_dynamic-update-slice_fusion), channel_id=1, source_target_pairs={{0,1},{1,2},{2,3},{3,0},{4,5},{5,6},{6,7},{7,4},{8,9},{9,10},{10,1... | collective-permute-start | bytes 122888 | tf_op jit(solution)/shard_map/ppermute | solution.py:15
  25.5 12.9 %all-to-all-start = ((bf16[32,80,128]{2,1,0:T(8,128)(2,1)}), bf16[32,80,128]{2,1,0:T(8,128)(2,1)S(1)}, u32[]{:S(2)}, u32[]{:S(2)}) async-start(bf16[32,80,128]{2,1,0:T(8,128)(2,1)} %bitcast.6), calls=%async_computation | async-start | bytes 1310720 | tf_op jit(solution)/shard_map/all_to_all | solution.py:147
  38.4 0.3 copy.45
  38.7 0.5 copy.33
  39.2 0.0 collective-permute-done.2
  39.2 0.0 collective-permute-done.1
  39.3 0.0 collective-permute-done
  39.3 0.9 fusion.5
  40.2 0.5 fusion.1
  40.7 0.1 copy.34
  40.8 0.2 fusion.6
  41.1 0.3 add_convert_fusion.l0
  41.3 4.4 %collective-permute-start.6 = (bf16[1280,128]{1,0:T(8,128)(2,1)S(1)}, bf16[1280,128]{1,0:T(8,128)(2,1)S(1)}, u32[]{:S(2)}, u32[]{:S(2)}) collective-permute-start(bf16[1280,128]{1,0:T(8,128)(2,1)S(1)} %bitcast.50), channel_id=1, source_target_pairs={{0,48},{16,0},{32,16},{48,32},{1,49},{17,1},{33,17},{49,33},{2,50}... | collective-permute-start | bytes 983048 | tf_op jit(solution)/shard_map/ppermute | solution.py:15
  45.7 2.5 %collective-permute-start.5 = (bf16[1280,128]{1,0:T(8,128)(2,1)S(1)}, bf16[1280,128]{1,0:T(8,128)(2,1)S(1)}, u32[]{:S(2)}, u32[]{:S(2)}) collective-permute-start(bf16[1280,128]{1,0:T(8,128)(2,1)S(1)} %bitcast.51), channel_id=1, source_target_pairs={{0,32},{16,48},{32,0},{48,16},{1,33},{17,49},{33,1},{49,17},{2,34}... | collective-permute-start | bytes 983048 | tf_op jit(solution)/shard_map/ppermute | solution.py:15
  48.2 2.5 %collective-permute-start.4 = (bf16[1280,128]{1,0:T(8,128)(2,1)S(1)}, bf16[1280,128]{1,0:T(8,128)(2,1)S(1)}, u32[]{:S(2)}, u32[]{:S(2)}) collective-permute-start(bf16[1280,128]{1,0:T(8,128)(2,1)S(1)} %bitcast.52), channel_id=1, source_target_pairs={{0,16},{16,32},{32,48},{48,0},{1,17},{17,33},{33,49},{49,1},{2,18}... | collective-permute-start | bytes 983048 | tf_op jit(solution)/shard_map/ppermute | solution.py:15
  50.7 4.8 %collective-permute-start.3 = (bf16[1280,128]{1,0:T(8,128)(2,1)S(1)}, bf16[1280,128]{1,0:T(8,128)(2,1)S(1)}, u32[]{:S(2)}, u32[]{:S(2)}) collective-permute-start(bf16[1280,128]{1,0:T(8,128)(2,1)S(1)} %bitcast.53), channel_id=1, source_target_pairs={{0,4},{4,0},{1,5},{5,1},{2,6},{6,2},{3,7},{7,3},{8,12},{12,8},{9,1... | collective-permute-start | bytes 983048 | tf_op jit(solution)/shard_map/ppermute | solution.py:163
  55.5 0.6 collective-permute-done.6
  56.1 4.5 %collective-permute-done.5 = bf16[1280,128]{1,0:T(8,128)(2,1)S(1)} collective-permute-done((bf16[1280,128]{1,0:T(8,128)(2,1)S(1)}, bf16[1280,128]{1,0:T(8,128)(2,1)S(1)}, u32[]{:S(2)}, u32[]{:S(2)}) %collective-permute-start.5) | collective-permute-done | bytes 327712 | tf_op jit(solution)/shard_map/ppermute | solution.py:15
  60.6 8.2 %collective-permute-done.4 = bf16[1280,128]{1,0:T(8,128)(2,1)S(1)} collective-permute-done((bf16[1280,128]{1,0:T(8,128)(2,1)S(1)}, bf16[1280,128]{1,0:T(8,128)(2,1)S(1)}, u32[]{:S(2)}, u32[]{:S(2)}) %collective-permute-start.4) | collective-permute-done | bytes 327712 | tf_op jit(solution)/shard_map/ppermute | solution.py:15
  68.8 0.0 collective-permute-done.3
  68.8 0.0 all-to-all-done
  68.8 0.0 all-gather.2.cloned.1.call-done.env_hbm
  68.9 1.3 %pad_maximum_fusion = bf16[6400,128]{1,0:T(8,128)(2,1)} fusion(bf16[1280,128]{1,0:T(8,128)(2,1)S(1)} %collective-permute-done.6, bf16[1280,128]{1,0:T(8,128)(2,1)S(1)} %collective-permute-done.5, bf16[1280,128]{1,0:T(8,128)(2,1)S(1)} %collective-permute-done.4, bf16[2560,128]{1,0:T(8,128)(2,1)S(1)} %bitcast.48), kind=kLoop, calls=%fused_computation | loop fusion | flops 6553600 | bytes 3276800 | tf_op jit(solution)/shard_map/concatenate | solution.py:165
  70.1 2.5 %collective-permute-start.7 = (bf16[6400,128]{1,0:T(8,128)(2,1)}, bf16[6400,128]{1,0:T(8,128)(2,1)}, u32[]{:S(2)}, u32[]{:S(2)}) collective-permute-start(bf16[6400,128]{1,0:T(8,128)(2,1)} %pad_maximum_fusion), channel_id=1, source_target_pairs={{0,4},{4,0},{1,5},{5,1},{2,6},{6,2},{3,7},{7,3},{8,12},{12,8},{9,1... | collective-permute-start | bytes 4915208 | tf_op jit(solution)/shard_map/ppermute | solution.py:165
  72.6 0.1 pad_add_fusion.place_ref
  72.7 0.1 constant_dynamic-slice_fusion
  72.8 0.1 copy.32
  72.9 0.1 copy.37.coef_ref
  73.0 3.1 %collective-permute-done.7 = bf16[6400,128]{1,0:T(8,128)(2,1)} collective-permute-done((bf16[6400,128]{1,0:T(8,128)(2,1)}, bf16[6400,128]{1,0:T(8,128)(2,1)}, u32[]{:S(2)}, u32[]{:S(2)}) %collective-permute-start.7) | collective-permute-done | bytes 1638432 | tf_op jit(solution)/shard_map/ppermute | solution.py:165
  76.1 1.3 %copy-done.1 = bf16[20,128,256]{2,1,0:T(8,128)(2,1)S(1)} copy-done((bf16[20,128,256]{2,1,0:T(8,128)(2,1)S(1)}, bf16[20,128,256]{2,1,0:T(8,128)(2,1)}, u32[]{:S(2)}) %copy-start.1) | copy-done | bytes 1310744
  77.4 10.5 %shard_map.73 = bf16[4,16,4,16,128]{4,3,2,1,0:T(8,128)(2,1)S(1)} custom-call(s32[3]{0:T(128)S(1)} %pad_add_fusion.place_ref, f32[20,48]{1,0:T(8,128)S(1)} %copy.37.coef_ref, bf16[20,128,256]{2,1,0:T(8,128)(2,1)S(1)} %copy-done.1, bf16[160,16,128]{2,1,0:T(8,128)(2,1)S(1)} %bitcast.49, bf16[400,16,128]{2,1,0:T(8,128)(2,1)} %bitcast.21.other_hbm, ...), custom_call_target="tpu_custom_call" | custom-call | flops 4200000000 | bytes 8000000 | tf_op jit(solution)/shard_map/pallas_call | solution.py:112
  87.9 0.0 copy-start.3
  87.9 16.1 %all_to_all.10 = bf16[4,16,4,16,128]{4,3,2,1,0:T(8,128)(2,1)S(1)} all-to-all(bf16[4,16,4,16,128]{4,3,2,1,0:T(8,128)(2,1)S(1)} %shard_map.73), channel_id=1, replica_groups=mesh['lrow'=8,'x1'=2,'x0'=2,'y'=2,'core'=2,'term'=4] {'x0','y'}, dimensions={0} | all-to-all | bytes 2097152 | tf_op jit(solution)/shard_map/all_to_all | solution.py:173
  104.0 0.2 convert_add_fusion
  104.2 0.0 copy-done.3
  104.2 1.0 fusion
  (22 shorter events, 0.1 us)
Async XLA Ops:
  6.5 1.1 copy-start
  6.5 4.4 %copy-start.6 = (bf16[5,4,256]{2,1,0:T(4,128)(2,1)S(1)}, bf16[5,4,256]{2,1,0:T(4,128)(2,1)}, u32[]{:S(2)}) copy-start(bf16[5,4,256]{2,1,0:T(4,128)(2,1)} %param.9) | copy-start | bytes 30724
  6.5 62.3 %all-gather.2.cloned.1.call-start = ((), (), s32[]{:S(2)}) async-start(), calls=%async_computation.2 | async-start | bytes 1638400 | tf_op jit(solution)/shard_map/all_gather | solution.py:139
  7.6 3.3 %copy-start.4 = (f32[5,3,128]{2,1,0:T(4,128)S(1)}, f32[5,3,128]{2,1,0:T(4,128)}, u32[]{:S(2)}) copy-start(f32[5,3,128]{2,1,0:T(4,128)} %param.11) | copy-start | bytes 23044
  7.6 3.4 %copy-start.5 = (f32[5,3,128]{2,1,0:T(4,128)S(1)}, f32[5,3,128]{2,1,0:T(4,128)}, u32[]{:S(2)}) copy-start(f32[5,3,128]{2,1,0:T(4,128)} %param.12) | copy-start | bytes 23044
  9.5 28.9 %copy-start.2 = (bf16[256,16,128]{2,1,0:T(8,128)(2,1)S(1)}, bf16[256,16,128]{2,1,0:T(8,128)(2,1)}, u32[]{:S(2)}) copy-start(bf16[256,16,128]{2,1,0:T(8,128)(2,1)} %param.7) | copy-start | bytes 3145732
  11.0 28.2 %collective-permute-start.2 = (f32[5,16,128]{2,0,1:T(8,128)S(1)}, f32[5,16,128]{2,0,1:T(8,128)S(1)}, u32[]{:S(2)}, u32[]{:S(2)}) collective-permute-start(f32[5,16,128]{2,0,1:T(8,128)S(1)} %constant_dynamic-update-slice_fusion), channel_id=1, source_target_pairs={{0,3},{1,0},{2,1},{3,2},{4,7},{5,4},{6,5},{7,6},{8,11},{9,8},{10,9... | collective-permute-start | bytes 122888 | tf_op jit(solution)/shard_map/ppermute | solution.py:15
  17.7 21.5 %collective-permute-start.1 = (f32[5,16,128]{2,0,1:T(8,128)S(1)}, f32[5,16,128]{2,0,1:T(8,128)}, u32[]{:S(2)}, u32[]{:S(2)}) collective-permute-start(f32[5,16,128]{2,0,1:T(8,128)S(1)} %constant_dynamic-update-slice_fusion), channel_id=1, source_target_pairs={{0,2},{1,3},{2,0},{3,1},{4,6},{5,7},{6,4},{7,5},{8,10},{9,11},{10,... | collective-permute-start | bytes 122888 | tf_op jit(solution)/shard_map/ppermute | solution.py:15
  21.3 18.0 %collective-permute-start = (f32[5,16,128]{2,0,1:T(8,128)S(1)}, f32[5,16,128]{2,0,1:T(8,128)}, u32[]{:S(2)}, u32[]{:S(2)}) collective-permute-start(f32[5,16,128]{2,0,1:T(8,128)S(1)} %constant_dynamic-update-slice_fusion), channel_id=1, source_target_pairs={{0,1},{1,2},{2,3},{3,0},{4,5},{5,6},{6,7},{7,4},{8,9},{9,10},{10,1... | collective-permute-start | bytes 122888 | tf_op jit(solution)/shard_map/ppermute | solution.py:15
  25.5 43.3 %all-to-all-start = ((bf16[32,80,128]{2,1,0:T(8,128)(2,1)}), bf16[32,80,128]{2,1,0:T(8,128)(2,1)S(1)}, u32[]{:S(2)}, u32[]{:S(2)}) async-start(bf16[32,80,128]{2,1,0:T(8,128)(2,1)} %bitcast.6), calls=%async_computation | async-start | bytes 1310720 | tf_op jit(solution)/shard_map/all_to_all | solution.py:147
  41.3 14.8 %collective-permute-start.6 = (bf16[1280,128]{1,0:T(8,128)(2,1)S(1)}, bf16[1280,128]{1,0:T(8,128)(2,1)S(1)}, u32[]{:S(2)}, u32[]{:S(2)}) collective-permute-start(bf16[1280,128]{1,0:T(8,128)(2,1)S(1)} %bitcast.50), channel_id=1, source_target_pairs={{0,48},{16,0},{32,16},{48,32},{1,49},{17,1},{33,17},{49,33},{2,50}... | collective-permute-start | bytes 983048 | tf_op jit(solution)/shard_map/ppermute | solution.py:15
  45.7 14.9 %collective-permute-start.5 = (bf16[1280,128]{1,0:T(8,128)(2,1)S(1)}, bf16[1280,128]{1,0:T(8,128)(2,1)S(1)}, u32[]{:S(2)}, u32[]{:S(2)}) collective-permute-start(bf16[1280,128]{1,0:T(8,128)(2,1)S(1)} %bitcast.51), channel_id=1, source_target_pairs={{0,32},{16,48},{32,0},{48,16},{1,33},{17,49},{33,1},{49,17},{2,34}... | collective-permute-start | bytes 983048 | tf_op jit(solution)/shard_map/ppermute | solution.py:15
  48.2 20.6 %collective-permute-start.4 = (bf16[1280,128]{1,0:T(8,128)(2,1)S(1)}, bf16[1280,128]{1,0:T(8,128)(2,1)S(1)}, u32[]{:S(2)}, u32[]{:S(2)}) collective-permute-start(bf16[1280,128]{1,0:T(8,128)(2,1)S(1)} %bitcast.52), channel_id=1, source_target_pairs={{0,16},{16,32},{32,48},{48,0},{1,17},{17,33},{33,49},{49,1},{2,18}... | collective-permute-start | bytes 983048 | tf_op jit(solution)/shard_map/ppermute | solution.py:15
  50.7 18.1 %collective-permute-start.3 = (bf16[1280,128]{1,0:T(8,128)(2,1)S(1)}, bf16[1280,128]{1,0:T(8,128)(2,1)S(1)}, u32[]{:S(2)}, u32[]{:S(2)}) collective-permute-start(bf16[1280,128]{1,0:T(8,128)(2,1)S(1)} %bitcast.53), channel_id=1, source_target_pairs={{0,4},{4,0},{1,5},{5,1},{2,6},{6,2},{3,7},{7,3},{8,12},{12,8},{9,1... | collective-permute-start | bytes 983048 | tf_op jit(solution)/shard_map/ppermute | solution.py:163
  70.1 6.0 %collective-permute-start.7 = (bf16[6400,128]{1,0:T(8,128)(2,1)}, bf16[6400,128]{1,0:T(8,128)(2,1)}, u32[]{:S(2)}, u32[]{:S(2)}) collective-permute-start(bf16[6400,128]{1,0:T(8,128)(2,1)} %pad_maximum_fusion), channel_id=1, source_target_pairs={{0,4},{4,0},{1,5},{5,1},{2,6},{6,2},{3,7},{7,3},{8,12},{12,8},{9,1... | collective-permute-start | bytes 4915208 | tf_op jit(solution)/shard_map/ppermute | solution.py:165
  76.1 1.3 %copy-start.1 = (bf16[20,128,256]{2,1,0:T(8,128)(2,1)S(1)}, bf16[20,128,256]{2,1,0:T(8,128)(2,1)}, u32[]{:S(2)}) copy-start(bf16[20,128,256]{2,1,0:T(8,128)(2,1)} %all-gather.2.cloned.1.call-done.env_hbm) | copy-start | bytes 3932164
  87.9 16.3 %copy-start.3 = (bf16[32,4,16,128]{3,2,1,0:T(8,128)(2,1)S(1)}, bf16[32,4,16,128]{3,2,1,0:T(8,128)(2,1)}, u32[]{:S(2)}) copy-start(bf16[32,4,16,128]{3,2,1,0:T(8,128)(2,1)} %param.13) | copy-start | bytes 1572868
Sparse Core Ops, SparseCore 0:
  9.5 46.7 all-gather.1

commit v3 on v2

v3 whole, which is shorter than its diff:
```python
import jax
import jax.numpy as jnp
from jax import lax
from jax.experimental import pallas as pl
from jax.experimental.pallas import tpu as pltpu
from jax.sharding import Mesh, PartitionSpec as P

BF16, F32 = jnp.bfloat16, jnp.float32
RCOL = ("x1", "x0", "y", "core")
VMEM = pl.BlockSpec(memory_space=pltpu.VMEM)
SMEM = pl.BlockSpec(memory_space=pltpu.SMEM)


def shifted(block, axes):
    return [lax.ppermute(block, axes, [(i, (i + shift) % 4) for i in range(4)]) for shift in range(1, 4)]


def unscramble(at, ref, core):
    lane = lax.broadcasted_iota(jnp.int32, (80, 128), 1)
    low, even = lane < 64, (lane // 32) % 2 == 0
    for x in range(4):
        for half in range(2):
            t0, t1, t2, t3 = (
                ref[((half * 4 + m) * 4 + x) * 5 : ((half * 4 + m) * 4 + x + 1) * 5].reshape(80, 128).astype(F32)
                for m in range(4)
            )
            t0, t2 = jnp.where(low, t0, pltpu.roll(t2, 64, 1)), jnp.where(low, pltpu.roll(t0, 64, 1), t2)
            t1, t3 = jnp.where(low, t1, pltpu.roll(t3, 64, 1)), jnp.where(low, pltpu.roll(t1, 64, 1), t3)
            t0, t1 = jnp.where(even, t0, pltpu.roll(t1, 32, 1)), jnp.where(even, pltpu.roll(t0, 96, 1), t1)
            t2, t3 = jnp.where(even, t2, pltpu.roll(t3, 32, 1)), jnp.where(even, pltpu.roll(t2, 96, 1), t3)
            for g, tile in enumerate((t0, t1, t2, t3)):
                tile = tile.astype(BF16)
                for jj in range(5):
                    j = jj * 4 + g
                    if j < 18:
                        top = j * 128 + at * 64 + x * 16
                        core[top : top + 16, half * 128 : half * 128 + 128] = tile[jj * 16 : jj * 16 + 16]


def frames_kernel(
    coef_ref, shared_hbm, mine_hbm, other_hbm, frame_hbm, token_ref, frame, env_ref, mine_ref, other_ref, core, raw, sem
):
    points, ranks, rows, group = 16, 128, 64, 4
    copies = [
        pltpu.make_async_copy(mine_hbm, mine_ref, sem.at[0]),
        pltpu.make_async_copy(other_hbm, other_ref, sem.at[1]),
    ]
    for t in range(4):
        for half in range(2):
            copies.append(
                pltpu.make_async_copy(
                    shared_hbm.at[t, pl.ds(half * 320, 320)],
                    env_ref.at[pl.ds(t * 320, 320), pl.ds(half * 128, 128)],
                    sem.at[2 + t * 2 + half],
                )
            )
    for copy in copies:
        copy.start()
    copies[0].wait()
    unscramble(0, mine_ref, core)
    copies[1].wait()
    unscramble(1, other_ref, core)
    for copy in copies[2:]:
        copy.wait()

    def make(step, carry):
        start = pl.multiple_of(step * group * rows, group * rows)
        env = env_ref[pl.ds(start, group * rows), :]
        raw[...] = lax.dot_general(env, core[...], (((1,), (1,)), ((), ())), preferred_element_type=F32)
        for at in range(group):
            t = step * group + at
            rows_at = slice(at * rows, (at + 1) * rows)
            columns = pl.ds(pl.multiple_of(t * ranks, ranks), ranks)
            for j in range(points):
                frame[j * rows : (j + 1) * rows, columns] = (
                    coef_ref[t, j] * raw[rows_at, (j + 1) * ranks : (j + 2) * ranks]
                    + coef_ref[t, points + j] * raw[rows_at, j * ranks : (j + 1) * ranks]
                    + coef_ref[t, 2 * points + j] * raw[rows_at, (j + 2) * ranks : (j + 3) * ranks]
                ).astype(BF16)
        out(step).start()
        return carry

    def out(step):
        columns = pl.ds(pl.multiple_of(step * group * ranks, group * ranks), group * ranks)
        return pltpu.make_async_copy(frame.at[:, columns], frame_hbm.at[:, columns], sem.at[10 + step])

    lax.fori_loop(0, 5, make, 0)
    token_ref[...] = raw[:8, :128]
    for step in range(5):
        out(step).wait()


def product_kernel(place_ref, frame_hbm, l0, l1, l2, l3, far_hbm, token, out_ref, left_ref, frame, sem):
    column = place_ref[0]
    pieces = []
    for shift, ref in enumerate((l0, l1, l2, l3)):
        top = pl.multiple_of(lax.rem(column - shift + 4, 4) * 16, 16)
        for a in range(4):
            lanes = pl.ds(a * 128, 128)
            for move, source in enumerate((ref, far_hbm.at[shift])):
                target = left_ref.at[:, pl.ds(top + move * 64, 16), lanes]
                pieces.append(pltpu.make_async_copy(source.at[a], target, sem.at[(shift * 4 + a) * 2 + move]))
    chunks = [
        pltpu.make_async_copy(frame_hbm.at[pl.ds(at * 256, 256)], frame.at[pl.ds(at * 256, 256)], sem.at[32 + at])
        for at in range(4)
    ]
    for copy in pieces + chunks:
        copy.start()
    for copy in pieces:
        copy.wait()

    def contract(step, carry):
        start = pl.multiple_of(step * 256, 256)
        pltpu.make_async_copy(frame_hbm.at[pl.ds(start, 256)], frame.at[pl.ds(start, 256)], sem.at[32 + step]).wait()
        part = jnp.dot(
            frame[pl.ds(start, 256), :], left_ref[...].reshape(2560, 512), preferred_element_type=F32
        ).astype(BF16)
        for at in range(4):
            for dest in range(4):
                top = at * 64 + dest * 16
                for a in range(4):
                    out_ref[dest, step * 4 + at, a] = part[top : top + 16, a * 128 : (a + 1) * 128]
        return carry

    lax.fori_loop(0, 4, contract, 0)


def left_kernel(shared_ref, core_ref, out_ref, coef_ref, tall):
    cores = jnp.swapaxes(core_ref[...].astype(F32), 0, 1).astype(BF16)
    lane = lax.broadcasted_iota(jnp.int32, (80, 128), 1)
    totals = []
    for t in range(4):
        total = (
            shared_ref[t, 680:710].astype(F32) + shared_ref[t, 710:740].astype(F32) + shared_ref[t, 740:770].astype(F32)
        )
        coef_ref[t] = total[15:]
        totals.append(total)
    envs = []
    for a in range(4):
        for t in range(4):
            rows = shared_ref[t, 640:680].astype(F32)
            envs.append(jnp.concatenate([rows[a * 5 : a * 5 + 5], rows[20 + a * 5 : 25 + a * 5]], axis=1))
    envs = jnp.concatenate(envs, axis=0).astype(BF16)
    scales = [[total[k * 5 : k * 5 + 5] for total in totals] * 4 for k in range(3)]
    centre, lower, upper = (jnp.concatenate(part, axis=0) for part in scales)
    lower = jnp.where(lane == 0, 0.0, lower)
    upper = jnp.where(lane == 127, 0.0, upper)
    for r in range(16):
        raw = jnp.dot(envs, cores[r], preferred_element_type=F32)
        tall[pl.ds(r, 80, stride=16), :] = (
            centre * raw + lower * pltpu.roll(raw, 1, 1) + upper * pltpu.roll(raw, 127, 1)
        )
    out_ref[...] = tall[...].astype(BF16)


def left_frames(shared, core):
    return pl.pallas_call(
        left_kernel,
        out_shape=(jax.ShapeDtypeStruct((1280, 128), BF16), jax.ShapeDtypeStruct((4, 15, 128), F32)),
        in_specs=[VMEM, VMEM],
        out_specs=(VMEM, VMEM),
        scratch_shapes=[pltpu.VMEM((1280, 128), F32)],
        compiler_params=pltpu.CompilerParams(vmem_limit_bytes=8 << 20),
        cost_estimate=pl.CostEstimate(flops=84_000_000, bytes_accessed=2_000_000, transcendentals=0),
    )(shared, core)


ANYWHERE = pl.BlockSpec(memory_space=pl.ANY)
HBM = pl.BlockSpec(memory_space=pltpu.HBM)


def right_frames(coef, shared, mine, other):
    return pl.pallas_call(
        frames_kernel,
        out_shape=(jax.ShapeDtypeStruct((1024, 2560), BF16), jax.ShapeDtypeStruct((8, 128), F32)),
        in_specs=[SMEM] + [ANYWHERE] * 3,
        out_specs=(HBM, VMEM),
        scratch_shapes=[
            pltpu.VMEM((1024, 2560), BF16),
            pltpu.VMEM((1280, 256), BF16),
            pltpu.VMEM((160, 16, 128), BF16),
            pltpu.VMEM((160, 16, 128), BF16),
            pltpu.VMEM((18 * 128, 256), BF16),
            pltpu.VMEM((256, 18 * 128), F32),
            pltpu.SemaphoreType.DMA((15,)),
        ],
        compiler_params=pltpu.CompilerParams(vmem_limit_bytes=52 << 20),
        cost_estimate=pl.CostEstimate(flops=1_500_000_000, bytes_accessed=8_000_000, transcendentals=0),
    )(coef, shared, mine, other)


def product(place, frame, pieces):
    return pl.pallas_call(
        product_kernel,
        out_shape=jax.ShapeDtypeStruct((4, 16, 4, 16, 128), BF16),
        in_specs=[SMEM, HBM] + [ANYWHERE] * 6,
        out_specs=VMEM,
        scratch_shapes=[
            pltpu.VMEM((20, 128, 512), BF16),
            pltpu.VMEM((1024, 2560), BF16),
            pltpu.SemaphoreType.DMA((36,)),
        ],
        compiler_params=pltpu.CompilerParams(vmem_limit_bytes=52 << 20),
        cost_estimate=pl.CostEstimate(flops=2_700_000_000, bytes_accessed=8_000_000, transcendentals=0),
    )(place, frame, *pieces)


def on_device(core_left, core_right, env_left, env_right, coef_left, coef_right, projected):
    x0, x1 = lax.axis_index("x0"), lax.axis_index("x1")
    core, term = lax.axis_index("core"), lax.axis_index("term")
    swap = [(0, 1), (1, 0)]

    env = env_right.reshape(5, 2, 4, 2, 16, 256)
    env = lax.dynamic_slice(env, (0, x1, 0, core, 0, 0), (5, 1, 4, 1, 16, 256)).reshape(320, 256)
    coefs = jnp.concatenate([coef_left.transpose(1, 0, 2).reshape(15, 128), coef_right.reshape(15, 128)])
    high = lax.reduce_precision(coefs, 8, 7)
    middle = lax.reduce_precision(coefs - high, 8, 7)
    low = coefs - high - middle
    envs = env_left.transpose(1, 0, 2).reshape(20, 256)
    shared = jnp.concatenate(
        [env[:, :128], env[:, 128:], envs[:, :128], envs[:, 128:]]
        + [part.astype(BF16) for part in (high, middle, low)]
        + [jnp.zeros((14, 128), BF16)]
    )
    shared = lax.all_gather(shared, "term")

    points = core_right.reshape(512, 128).T
    points = jnp.pad(points, ((1, 3), (0, 0)))
    mine = lax.dynamic_slice(points, (term * 32, 0), (36, 512))
    windows = jnp.stack([mine[:20], mine[16:]]).reshape(2, 5, 4, 16, 32).transpose(0, 1, 3, 2, 4)
    windows = jnp.broadcast_to(windows.reshape(1, 2, 80, 128), (16, 2, 80, 128)).reshape(32, 80, 128)
    slices = lax.all_to_all(windows, ("lrow", "x1", "x0"), 0, 0, tiled=True).reshape(2560, 128)

    left, rights = left_frames(shared, core_left)
    others = shifted(left, ("x1", "x0"))
    slices, left = lax.optimization_barrier((slices, left))
    other = lax.ppermute(slices, "core", swap)
    coef = lax.dynamic_slice(rights.reshape(20, 3, 128), (0, 0, term * 32 + x0 * 16), (20, 3, 16)).reshape(20, 48)
    frame, token = right_frames(coef, shared, slices.reshape(160, 16, 128), other.reshape(160, 16, 128))
    token, others = lax.optimization_barrier((token, others))
    twins = lax.ppermute(jnp.concatenate([left] + others), "core", swap).reshape(4, 4, 20, 16, 128)
    pieces = [piece.reshape(4, 20, 16, 128) for piece in [left] + others]
    part = product((x1 * 2 + x0).reshape(1), frame, pieces + [twins, token])
    part = lax.all_to_all(part, ("x0", "y"), 0, 0, tiled=True).reshape(2, 2, 16, 4, 16, 128)
    summed = (part[:, 0].astype(F32) + part[:, 1].astype(F32)).reshape(32, 4, 16, 128)
    return (projected.astype(F32) - summed).astype(BF16)


def solution(mesh):
    split = Mesh(mesh.devices.reshape(8, 2, 2, 2, 2, 4), ("lrow",) + RCOL + ("term",))
    return jax.shard_map(
        on_device,
        mesh=split,
        in_specs=(
            P(None, RCOL, None),
            P(RCOL, "lrow", None),
            P("term", "lrow", None),
            P("term", None, None),
            P("term", None, None),
            P("term", None, None),
            P("term", "lrow", RCOL, None),
        ),
        out_specs=P("term", "lrow", RCOL, None),
        check_vma=False,
    )
```

time: 113 us -> 99.9 us (0.88)
  blocking collectives: 16.1 us -> 35.7 us
  between operations: 13.7 us -> 0.35 us
  starting transfers between devices: 44 us -> 32.3 us
  waiting for transfers between devices: 16.5 us -> 9.98 us
  Pallas kernels: 10.5 us -> 15.4 us
  local copies, waits for them, and re-layouts: 7.02 us -> 3.42 us
  other arithmetic: 3.74 us -> 2.35 us
    all_gather x0 -> x1, blocking collectives: none -> 18.5 us  [on_device(): shared = lax.all_gather(shared, 'term')]
    ppermute x6 -> x3, starting transfers between devices: 23.8 us -> 9.38 us  [shifted(): lax.ppermute(block, axes, [(i, (i + shift) % 4) for i in range(4)])]
    ppermute x6 -> x3, waiting for transfers between devices: 13.3 us -> 7 us  [shifted(): lax.ppermute(block, axes, [(i, (i + shift) % 4) for i in range(4)])]
    pallas_call x1 -> x3, Pallas kernels: 10.5 us -> 15.4 us  [the longest x1 7.75 us: right_frames(): pl.pallas_call(frames_kernel, out_shape=(jax.ShapeDtypeStruct((1024, 2560...]
    unnamed x20 -> x14, local copies, waits for them, and re-layouts: 2.71 us -> 0.03 us
    ppermute x2, starting transfers between devices: 7.32 us -> 9.19 us  [the longest x1 6.79 us: on_device(): other = lax.ppermute(slices, 'core', swap)]
  transfers between devices with their start and end apart: 10 -> 6, of which waited for: 4 -> 3; matrix products, arithmetic and copies ran while one was open for 5% -> 1% of each run, Pallas kernels for 0% -> 9%
where the time goes in v3:
time: 99.9 us; the launch traced here: 99.4 us
  blocking collectives  35.7 us (36%)
  starting transfers between devices  32.3 us (32%)
  Pallas kernels  15.4 us (15%)
  waiting for transfers between devices  9.98 us (10%)
  local copies, waits for them, and re-layouts  3.42 us (3%)
  other arithmetic  2.35 us (2%)
    all_gather x1, blocking collectives, on_device(): shared = lax.all_gather(shared, 'term')  18.5 us
    all_to_all x1, blocking collectives, on_device(): lax.all_to_all(part, ('x0', 'y'), 0, 0, tiled=True)  17.2 us
    all_to_all x1, starting transfers between devices, on_device(): lax.all_to_all(windows, ('lrow', 'x1', 'x0'), 0, 0, tiled=True)  13.7 us
    ppermute x3, starting transfers between devices, shifted(): lax.ppermute(block, axes, [(i, (i + shift) % 4) for i in range(4)])  9.38 us
    pallas_call x1, Pallas kernels, right_frames(): pl.pallas_call(frames_kernel, out_shape=(jax.ShapeDtypeStruct((1024, 2560...  7.75 us
    ppermute x3, waiting for transfers between devices, shifted(): lax.ppermute(block, axes, [(i, (i + shift) % 4) for i in range(4)])  7 us
    ppermute x1, starting transfers between devices, on_device(): other = lax.ppermute(slices, 'core', swap)  6.79 us
    pallas_call x1, Pallas kernels, product(): pl.pallas_call(product_kernel, out_shape=jax.ShapeDtypeStruct((4, 16, 4,...  6.55 us
  transfers between devices with their start and end apart: 6, of which 3 were waited for; matrix products, arithmetic and copies ran while one was open for 1% of the time, Pallas kernels for 9%

profile of v3, /device:TPU:1, one launch (start us, length us, event | category | flops | bytes accessed | tf_op | source)
XLA Modules:
  0.0 99.4 jit_solution(13302464672543776277)
XLA Ops:
  0.0 0.0 copy-start
  0.0 0.0 copy-start.4
  0.0 0.0 copy-start.5
  0.0 0.0 copy-start.6
  0.0 1.1 %copy.11 = bf16[512,128]{0,1:T(8,128)(2,1)S(1)} copy(bf16[512,128]{1,0:T(8,128)(2,1)} %bitcast.37) | data formatting | bytes 262144 | tf_op jit(solution)/shard_map/reshape | solution.py:227
  1.2 0.1 stack.9
  1.3 0.0 copy-start.2
  1.3 0.1 stack.10
  1.4 0.1 copy.12
  1.5 0.1 broadcast_in_dim.11
  1.7 0.9 broadcast_in_dim.12
  2.6 13.7 %all-to-all-start = ((bf16[32,80,128]{2,1,0:T(8,128)(2,1)}), bf16[32,80,128]{2,1,0:T(8,128)(2,1)S(1)}, u32[]{:S(2)}, u32[]{:S(2)}) async-start(bf16[32,80,128]{2,1,0:T(8,128)(2,1)} %bitcast.10), calls=%async_computation | async-start | bytes 1310720 | tf_op jit(solution)/shard_map/all_to_all | solution.py:232
  16.3 0.0 copy-done.4
  16.4 0.0 copy-done.5
  16.4 0.0 copy-done.6
  16.4 0.0 copy-done
  16.5 0.6 concatenate.11
  17.1 18.5 %all-gather = bf16[3136,128]{1,0:T(8,128)(2,1)S(1)} all-gather(bf16[784,128]{1,0:T(8,128)(2,1)S(1)} %concatenate.11), channel_id=2, replica_groups=mesh['lrow'=8,'x1'=2,'x0'=2,'y'=2,'core'=2,'term'=4] {'term'}, dimensions={0}, use_global_device_ids=true | all-gather | bytes 1003520 | tf_op jit(solution)/shard_map/all_gather | solution.py:225
  35.7 0.0 copy-start.1
  35.7 0.0 copy-done.2
  35.7 1.1 %shard_map.73 = (bf16[1280,128]{1,0:T(8,128)(2,1)S(1)}, f32[4,15,128]{2,1,0:T(8,128)S(1)}) custom-call(bf16[4,784,128]{2,1,0:T(8,128)(2,1)S(1)} %bitcast.26, bf16[256,16,128]{2,1,0:T(8,128)(2,1)S(1)} %copy-done.2), custom_call_target="tpu_custom_call" | custom-call | flops 84000000 | bytes 2000000 | tf_op jit(solution)/shard_map/pallas_call | solution.py:157
  36.7 0.0 all-to-all-done
  36.7 6.8 %collective-permute-start = (bf16[2560,128]{1,0:T(8,128)(2,1)S(1)}, bf16[2560,128]{1,0:T(8,128)(2,1)}, u32[]{:S(2)}, u32[]{:S(2)}) collective-permute-start(bf16[2560,128]{1,0:T(8,128)(2,1)S(1)} %bitcast.28), channel_id=1, source_target_pairs={{0,4},{4,0},{1,5},{5,1},{2,6},{6,2},{3,7},{7,3},{8,12},{12,8},{9,1... | collective-permute-start | bytes 1966088 | tf_op jit(solution)/shard_map/ppermute | solution.py:237
  43.5 4.4 %collective-permute-start.3 = (bf16[1280,128]{1,0:T(8,128)(2,1)S(1)}, bf16[1280,128]{1,0:T(8,128)(2,1)S(1)}, u32[]{:S(2)}, u32[]{:S(2)}) collective-permute-start(bf16[1280,128]{1,0:T(8,128)(2,1)S(1)} %get-tuple-element.19), channel_id=1, source_target_pairs={{0,48},{16,0},{32,16},{48,32},{1,49},{17,1},{33,17},{49,33},{2,50}... | collective-permute-start | bytes 983048 | tf_op jit(solution)/shard_map/ppermute | solution.py:15
  47.9 2.4 %collective-permute-start.2 = (bf16[1280,128]{1,0:T(8,128)(2,1)S(1)}, bf16[1280,128]{1,0:T(8,128)(2,1)S(1)}, u32[]{:S(2)}, u32[]{:S(2)}) collective-permute-start(bf16[1280,128]{1,0:T(8,128)(2,1)S(1)} %get-tuple-element.19), channel_id=1, source_target_pairs={{0,32},{16,48},{32,0},{48,16},{1,33},{17,49},{33,1},{49,17},{2,34}... | collective-permute-start | bytes 983048 | tf_op jit(solution)/shard_map/ppermute | solution.py:15
  50.3 2.6 %collective-permute-start.1 = (bf16[1280,128]{1,0:T(8,128)(2,1)S(1)}, bf16[1280,128]{1,0:T(8,128)(2,1)S(1)}, u32[]{:S(2)}, u32[]{:S(2)}) collective-permute-start(bf16[1280,128]{1,0:T(8,128)(2,1)S(1)} %get-tuple-element.19), channel_id=1, source_target_pairs={{0,16},{16,32},{32,48},{48,0},{1,17},{17,33},{33,49},{49,1},{2,18}... | collective-permute-start | bytes 983048 | tf_op jit(solution)/shard_map/ppermute | solution.py:15
  53.0 0.1 constant_dynamic-slice_fusion
  53.1 0.1 copy.10
  53.2 0.1 copy.13.coef_ref
  53.2 0.0 collective-permute-done
  53.2 0.0 copy-done.1
  53.2 7.7 %shard_map.74 = (bf16[1024,2560]{1,0:T(8,128)(2,1)}, f32[8,128]{1,0:T(8,128)S(1)}) custom-call(f32[20,48]{1,0:T(8,128)S(1)} %copy.13.coef_ref, bf16[4,784,128]{2,1,0:T(8,128)(2,1)} %bitcast.27, bf16[160,16,128]{2,1,0:T(8,128)(2,1)S(1)} %bitcast.29, bf16[160,16,128]{2,1,0:T(8,128)(2,1)} %bitcast.13.other_hbm), custom_call_target="tpu_custom_call" | custom-call | flops 1500000000 | bytes 8000000 | tf_op jit(solution)/shard_map/pallas_call | solution.py:173
  61.0 0.9 collective-permute-done.3
  61.9 0.0 collective-permute-done.2
  61.9 6.1 %collective-permute-done.1 = bf16[1280,128]{1,0:T(8,128)(2,1)S(1)} collective-permute-done((bf16[1280,128]{1,0:T(8,128)(2,1)S(1)}, bf16[1280,128]{1,0:T(8,128)(2,1)S(1)}, u32[]{:S(2)}, u32[]{:S(2)}) %collective-permute-start.1) | collective-permute-done | bytes 327712 | tf_op jit(solution)/shard_map/ppermute | solution.py:15
  68.0 1.2 %pad_maximum_fusion = bf16[5120,128]{1,0:T(8,128)(2,1)} fusion(bf16[1280,128]{1,0:T(8,128)(2,1)S(1)} %collective-permute-done.3, bf16[1280,128]{1,0:T(8,128)(2,1)S(1)} %collective-permute-done.2, bf16[1280,128]{1,0:T(8,128)(2,1)S(1)} %collective-permute-done.1, bf16[1280,128]{1,0:T(8,128)(2,1)S(1)} %get-tuple-element.19), kind=kLoop, calls=%fused_computation | loop fusion | flops 5242880 | bytes 2621440 | tf_op jit(solution)/shard_map/concatenate | solution.py:241
  69.2 2.4 %collective-permute-start.4 = (bf16[5120,128]{1,0:T(8,128)(2,1)}, bf16[5120,128]{1,0:T(8,128)(2,1)}, u32[]{:S(2)}, u32[]{:S(2)}) collective-permute-start(bf16[5120,128]{1,0:T(8,128)(2,1)} %pad_maximum_fusion), channel_id=1, source_target_pairs={{0,4},{4,0},{1,5},{5,1},{2,6},{6,2},{3,7},{7,3},{8,12},{12,8},{9,1... | collective-permute-start | bytes 3932168 | tf_op jit(solution)/shard_map/ppermute | solution.py:241
  71.6 3.0 %collective-permute-done.4 = bf16[5120,128]{1,0:T(8,128)(2,1)} collective-permute-done((bf16[5120,128]{1,0:T(8,128)(2,1)}, bf16[5120,128]{1,0:T(8,128)(2,1)}, u32[]{:S(2)}, u32[]{:S(2)}) %collective-permute-start.4) | collective-permute-done | bytes 1310752 | tf_op jit(solution)/shard_map/ppermute | solution.py:241
  74.5 6.6 %shard_map.75 = bf16[4,16,4,16,128]{4,3,2,1,0:T(8,128)(2,1)} custom-call(s32[1]{0:T(128)} %bitcast.place_ref, bf16[1024,2560]{1,0:T(8,128)(2,1)} %get-tuple-element.18.frame_hbm, bf16[4,20,16,128]{3,2,1,0:T(8,128)(2,1)S(1)} %bitcast.30, bf16[4,20,16,128]{3,2,1,0:T(8,128)(2,1)S(1)} %bitcast.33, bf16[4,20,16,128]{3,2,1,0:T(8,128)(2,1)S(1)} %bitcast.32, ...), custom_call_target="tpu_custom_call" | custom-call | flops 2700000000 | bytes 8000000 | tf_op jit(solution)/shard_map/pallas_call | solution.py:193
  81.1 0.0 copy-start.3
  81.1 17.2 %all_to_all.10 = bf16[4,16,4,16,128]{4,3,2,1,0:T(8,128)(2,1)S(1)} all-to-all(bf16[4,16,4,16,128]{4,3,2,1,0:T(8,128)(2,1)} %shard_map.75), channel_id=1, replica_groups=mesh['lrow'=8,'x1'=2,'x0'=2,'y'=2,'core'=2,'term'=4] {'x0','y'}, dimensions={0} | all-to-all | bytes 2097152 | tf_op jit(solution)/shard_map/all_to_all | solution.py:244
  98.3 0.2 convert_add_fusion
  98.5 0.0 copy-done.3
  98.5 1.0 fusion
  (13 shorter events, 0.2 us)
Async XLA Ops:
  0.0 16.4 %copy-start = (bf16[5,256,256]{2,1,0:T(8,128)(2,1)S(1)}, bf16[5,256,256]{2,1,0:T(8,128)(2,1)}, u32[]{:S(2)}) copy-start(bf16[5,256,256]{2,1,0:T(8,128)(2,1)} %param.10) | copy-start | bytes 1966084
  0.0 16.3 %copy-start.4 = (f32[5,3,128]{2,1,0:T(4,128)S(1)}, f32[5,3,128]{2,1,0:T(4,128)}, u32[]{:S(2)}) copy-start(f32[5,3,128]{2,1,0:T(4,128)} %param.12) | copy-start | bytes 23044
  0.0 16.3 %copy-start.5 = (f32[5,3,128]{2,1,0:T(4,128)S(1)}, f32[5,3,128]{2,1,0:T(4,128)}, u32[]{:S(2)}) copy-start(f32[5,3,128]{2,1,0:T(4,128)} %param.11) | copy-start | bytes 23044
  0.0 16.4 %copy-start.6 = (bf16[5,4,256]{2,1,0:T(4,128)(2,1)S(1)}, bf16[5,4,256]{2,1,0:T(4,128)(2,1)}, u32[]{:S(2)}) copy-start(bf16[5,4,256]{2,1,0:T(4,128)(2,1)} %param.9) | copy-start | bytes 30724
  1.3 34.4 %copy-start.2 = (bf16[256,16,128]{2,1,0:T(8,128)(2,1)S(1)}, bf16[256,16,128]{2,1,0:T(8,128)(2,1)}, u32[]{:S(2)}) copy-start(bf16[256,16,128]{2,1,0:T(8,128)(2,1)} %core_ref.1) | copy-start | bytes 3145732
  2.6 34.1 %all-to-all-start = ((bf16[32,80,128]{2,1,0:T(8,128)(2,1)}), bf16[32,80,128]{2,1,0:T(8,128)(2,1)S(1)}, u32[]{:S(2)}, u32[]{:S(2)}) async-start(bf16[32,80,128]{2,1,0:T(8,128)(2,1)} %bitcast.10), calls=%async_computation | async-start | bytes 1310720 | tf_op jit(solution)/shard_map/all_to_all | solution.py:232
  35.7 17.6 %copy-start.1 = (bf16[3136,128]{1,0:T(8,128)(2,1)}, bf16[3136,128]{1,0:T(8,128)(2,1)S(1)}, u32[]{:S(2)}) copy-start(bf16[3136,128]{1,0:T(8,128)(2,1)S(1)} %all-gather) | copy-start | bytes 2408452
  36.7 16.5 %collective-permute-start = (bf16[2560,128]{1,0:T(8,128)(2,1)S(1)}, bf16[2560,128]{1,0:T(8,128)(2,1)}, u32[]{:S(2)}, u32[]{:S(2)}) collective-permute-start(bf16[2560,128]{1,0:T(8,128)(2,1)S(1)} %bitcast.28), channel_id=1, source_target_pairs={{0,4},{4,0},{1,5},{5,1},{2,6},{6,2},{3,7},{7,3},{8,12},{12,8},{9,1... | collective-permute-start | bytes 1966088 | tf_op jit(solution)/shard_map/ppermute | solution.py:237
  43.5 18.4 %collective-permute-start.3 = (bf16[1280,128]{1,0:T(8,128)(2,1)S(1)}, bf16[1280,128]{1,0:T(8,128)(2,1)S(1)}, u32[]{:S(2)}, u32[]{:S(2)}) collective-permute-start(bf16[1280,128]{1,0:T(8,128)(2,1)S(1)} %get-tuple-element.19), channel_id=1, source_target_pairs={{0,48},{16,0},{32,16},{48,32},{1,49},{17,1},{33,17},{49,33},{2,50}... | collective-permute-start | bytes 983048 | tf_op jit(solution)/shard_map/ppermute | solution.py:15
  47.9 14.0 %collective-permute-start.2 = (bf16[1280,128]{1,0:T(8,128)(2,1)S(1)}, bf16[1280,128]{1,0:T(8,128)(2,1)S(1)}, u32[]{:S(2)}, u32[]{:S(2)}) collective-permute-start(bf16[1280,128]{1,0:T(8,128)(2,1)S(1)} %get-tuple-element.19), channel_id=1, source_target_pairs={{0,32},{16,48},{32,0},{48,16},{1,33},{17,49},{33,1},{49,17},{2,34}... | collective-permute-start | bytes 983048 | tf_op jit(solution)/shard_map/ppermute | solution.py:15
  50.3 17.7 %collective-permute-start.1 = (bf16[1280,128]{1,0:T(8,128)(2,1)S(1)}, bf16[1280,128]{1,0:T(8,128)(2,1)S(1)}, u32[]{:S(2)}, u32[]{:S(2)}) collective-permute-start(bf16[1280,128]{1,0:T(8,128)(2,1)S(1)} %get-tuple-element.19), channel_id=1, source_target_pairs={{0,16},{16,32},{32,48},{48,0},{1,17},{17,33},{33,49},{49,1},{2,18}... | collective-permute-start | bytes 983048 | tf_op jit(solution)/shard_map/ppermute | solution.py:15
  69.2 5.4 %collective-permute-start.4 = (bf16[5120,128]{1,0:T(8,128)(2,1)}, bf16[5120,128]{1,0:T(8,128)(2,1)}, u32[]{:S(2)}, u32[]{:S(2)}) collective-permute-start(bf16[5120,128]{1,0:T(8,128)(2,1)} %pad_maximum_fusion), channel_id=1, source_target_pairs={{0,4},{4,0},{1,5},{5,1},{2,6},{6,2},{3,7},{7,3},{8,12},{12,8},{9,1... | collective-permute-start | bytes 3932168 | tf_op jit(solution)/shard_map/ppermute | solution.py:241
  81.1 17.4 %copy-start.3 = (bf16[32,4,16,128]{3,2,1,0:T(8,128)(2,1)S(1)}, bf16[32,4,16,128]{3,2,1,0:T(8,128)(2,1)}, u32[]{:S(2)}) copy-start(bf16[32,4,16,128]{3,2,1,0:T(8,128)(2,1)} %param.13) | copy-start | bytes 1572868

commit v4 on v3

--- a/solution.py
+++ b/solution.py
@@ -9,10 +9,6 @@
 RCOL = ("x1", "x0", "y", "core")
 VMEM = pl.BlockSpec(memory_space=pltpu.VMEM)
 SMEM = pl.BlockSpec(memory_space=pltpu.SMEM)
-
-
-def shifted(block, axes):
-    return [lax.ppermute(block, axes, [(i, (i + shift) % 4) for i in range(4)]) for shift in range(1, 4)]
 
 
 def unscramble(at, ref, core):
@@ -90,16 +86,13 @@
         out(step).wait()
 
 
-def product_kernel(place_ref, frame_hbm, l0, l1, l2, l3, far_hbm, token, out_ref, left_ref, frame, sem):
-    column = place_ref[0]
+def product_kernel(frame_hbm, mine_hbm, twin_hbm, token, out_ref, left_ref, frame, sem):
     pieces = []
-    for shift, ref in enumerate((l0, l1, l2, l3)):
-        top = pl.multiple_of(lax.rem(column - shift + 4, 4) * 16, 16)
+    for x in range(4):
         for a in range(4):
-            lanes = pl.ds(a * 128, 128)
-            for move, source in enumerate((ref, far_hbm.at[shift])):
-                target = left_ref.at[:, pl.ds(top + move * 64, 16), lanes]
-                pieces.append(pltpu.make_async_copy(source.at[a], target, sem.at[(shift * 4 + a) * 2 + move]))
+            for move, source in enumerate((mine_hbm, twin_hbm)):
+                target = left_ref.at[:, pl.ds(move * 64 + x * 16, 16), pl.ds(a * 128, 128)]
+                pieces.append(pltpu.make_async_copy(source.at[x, a], target, sem.at[(x * 4 + a) * 2 + move]))
     chunks = [
         pltpu.make_async_copy(frame_hbm.at[pl.ds(at * 256, 256)], frame.at[pl.ds(at * 256, 256)], sem.at[32 + at])
         for at in range(4)
@@ -189,11 +182,11 @@
     )(coef, shared, mine, other)
 
 
-def product(place, frame, pieces):
+def product(frame, mine, twin, token):
     return pl.pallas_call(
         product_kernel,
         out_shape=jax.ShapeDtypeStruct((4, 16, 4, 16, 128), BF16),
-        in_specs=[SMEM, HBM] + [ANYWHERE] * 6,
+        in_specs=[HBM] + [ANYWHERE] * 3,
         out_specs=VMEM,
         scratch_shapes=[
             pltpu.VMEM((20, 128, 512), BF16),
@@ -202,7 +195,7 @@
         ],
         compiler_params=pltpu.CompilerParams(vmem_limit_bytes=52 << 20),
         cost_estimate=pl.CostEstimate(flops=2_700_000_000, bytes_accessed=8_000_000, transcendentals=0),
-    )(place, frame, *pieces)
+    )(frame, mine, twin, token)
 
 
 def on_device(core_left, core_right, env_left, env_right, coef_left, coef_right, projected):
@@ -232,15 +225,14 @@
     slices = lax.all_to_all(windows, ("lrow", "x1", "x0"), 0, 0, tiled=True).reshape(2560, 128)
 
     left, rights = left_frames(shared, core_left)
-    others = shifted(left, ("x1", "x0"))
+    lefts = lax.all_to_all(jnp.broadcast_to(left[None], (4, 1280, 128)), ("x1", "x0"), 0, 0, tiled=True)
     slices, left = lax.optimization_barrier((slices, left))
     other = lax.ppermute(slices, "core", swap)
     coef = lax.dynamic_slice(rights.reshape(20, 3, 128), (0, 0, term * 32 + x0 * 16), (20, 3, 16)).reshape(20, 48)
     frame, token = right_frames(coef, shared, slices.reshape(160, 16, 128), other.reshape(160, 16, 128))
-    token, others = lax.optimization_barrier((token, others))
-    twins = lax.ppermute(jnp.concatenate([left] + others), "core", swap).reshape(4, 4, 20, 16, 128)
-    pieces = [piece.reshape(4, 20, 16, 128) for piece in [left] + others]
-    part = product((x1 * 2 + x0).reshape(1), frame, pieces + [twins, token])
+    token, lefts = lax.optimization_barrier((token, lefts))
+    twins = lax.ppermute(lefts, "core", swap)
+    part = product(frame, lefts.reshape(4, 4, 20, 16, 128), twins.reshape(4, 4, 20, 16, 128), token)
     part = lax.all_to_all(part, ("x0", "y"), 0, 0, tiled=True).reshape(2, 2, 16, 4, 16, 128)
     summed = (part[:, 0].astype(F32) + part[:, 1].astype(F32)).reshape(32, 4, 16, 128)
     return (projected.astype(F32) - summed).astype(BF16)

time: 99.9 us -> 91.6 us (0.917)
  waiting for transfers between devices: 9.98 us -> 4.26 us
  local copies, waits for them, and re-layouts: 3.42 us -> 6.6 us
  starting transfers between devices: 32.3 us -> 29.4 us
  blocking collectives: 35.7 us -> 34.5 us
  other arithmetic: 2.35 us -> 1.19 us
    ppermute x4 -> x1, starting transfers between devices: 11.8 us -> 4.62 us  [on_device(): twins = lax.ppermute(lefts, 'core', swap)]
    ppermute x4 -> x1, waiting for transfers between devices: 9.97 us -> 2.85 us  [on_device(): twins = lax.ppermute(lefts, 'core', swap)]
    all_to_all x0 -> x1, starting transfers between devices: none -> 4.3 us  [on_device(): lax.all_to_all(jnp.broadcast_to(left[None], (4, 1280, 128)), ('x1', 'x0')...]
    unnamed x14 -> x16, local copies, waits for them, and re-layouts: 0.03 us -> 1.96 us
    ppermute x1, waiting for transfers between devices: 0.01 us -> 1.41 us  [on_device(): other = lax.ppermute(slices, 'core', swap)]
    broadcast_in_dim x0 -> x1, local copies, waits for them, and re-layouts: none -> 1.24 us  [on_device(): jnp.broadcast_to(left[None], (4, 1280, 128))]
    all_to_all x1, blocking collectives: 17.2 us -> 16 us  [on_device(): lax.all_to_all(part, ('x0', 'y'), 0, 0, tiled=True)]
    concatenate x1 -> x0, other arithmetic: 1.16 us -> none  [on_device(): jnp.concatenate([left] + others)]
  transfers between devices with their start and end apart: 6 -> 4, of which waited for: 3 -> 2; matrix products, arithmetic and copies ran while one was open for 1% -> 1% of each run, Pallas kernels for 9% -> 10%
where the time goes in v4:
time: 91.6 us; the launch traced here: 90.9 us
  blocking collectives  34.5 us (38%)
  starting transfers between devices  29.4 us (32%)
  Pallas kernels  14.6 us (16%)
  local copies, waits for them, and re-layouts  6.6 us (7%)
  waiting for transfers between devices  4.26 us (5%)
  other arithmetic  1.19 us (1%)
    all_gather x1, blocking collectives, on_device(): shared = lax.all_gather(shared, 'term')  18.5 us
    all_to_all x1, blocking collectives, on_device(): lax.all_to_all(part, ('x0', 'y'), 0, 0, tiled=True)  16 us
    all_to_all x1, starting transfers between devices, on_device(): lax.all_to_all(windows, ('lrow', 'x1', 'x0'), 0, 0, tiled=True)  13.7 us
    pallas_call x1, Pallas kernels, right_frames(): pl.pallas_call(frames_kernel, out_shape=(jax.ShapeDtypeStruct((1024, 2560...  7.65 us
    ppermute x1, starting transfers between devices, on_device(): other = lax.ppermute(slices, 'core', swap)  6.82 us
    pallas_call x1, Pallas kernels, product(): pl.pallas_call(product_kernel, out_shape=jax.ShapeDtypeStruct((4, 16, 4,...  5.92 us
    ppermute x1, starting transfers between devices, on_device(): twins = lax.ppermute(lefts, 'core', swap)  4.62 us
    all_to_all x1, starting transfers between devices, on_device(): lax.all_to_all(jnp.broadcast_to(left[None], (4, 1280, 128)), ('x1', 'x0')...  4.3 us
  transfers between devices with their start and end apart: 4, of which 2 were waited for; matrix products, arithmetic and copies ran while one was open for 1% of the time, Pallas kernels for 10%

profile of v4, /device:TPU:1, one launch (start us, length us, event | category | flops | bytes accessed | tf_op | source)
XLA Modules:
  0.0 90.9 jit_solution(8642597417284460100)
XLA Ops:
  0.0 0.0 copy-start
  0.0 1.1 %copy.11 = bf16[512,128]{0,1:T(8,128)(2,1)S(1)} copy(bf16[512,128]{1,0:T(8,128)(2,1)} %bitcast.30) | data formatting | bytes 262144 | tf_op jit(solution)/shard_map/reshape | solution.py:220
  1.1 0.1 stack.9
  1.3 0.1 stack.10
  1.4 0.0 copy-start.4
  1.4 0.0 copy-start.5
  1.4 0.0 copy-start.6
  1.4 0.1 copy.12
  1.5 0.1 broadcast_in_dim.17
  1.7 0.9 %broadcast_in_dim.18 = bf16[16,2,80,128]{3,2,1,0:T(8,128)(2,1)} broadcast(bf16[2,80,128]{2,1,0:T(8,128)(2,1)S(1)} %broadcast_in_dim.17), dimensions={1,2,3} | broadcast | bytes 696320 | tf_op jit(solution)/shard_map/broadcast_in_dim | solution.py:224
  2.6 13.7 %all-to-all-start = ((bf16[32,80,128]{2,1,0:T(8,128)(2,1)}), bf16[32,80,128]{2,1,0:T(8,128)(2,1)S(1)}, u32[]{:S(2)}, u32[]{:S(2)}) async-start(bf16[32,80,128]{2,1,0:T(8,128)(2,1)} %bitcast.9), calls=%async_computation | async-start | bytes 1310720 | tf_op jit(solution)/shard_map/all_to_all | solution.py:225
  16.3 0.0 copy-start.2
  16.3 0.0 copy-done.4
  16.4 0.0 copy-done.5
  16.4 0.0 copy-done.6
  16.5 0.0 copy-done
  16.5 0.6 concatenate.8
  17.1 18.5 %all-gather = bf16[3136,128]{1,0:T(8,128)(2,1)S(1)} all-gather(bf16[784,128]{1,0:T(8,128)(2,1)S(1)} %concatenate.8), channel_id=2, replica_groups=mesh['lrow'=8,'x1'=2,'x0'=2,'y'=2,'core'=2,'term'=4] {'term'}, dimensions={0}, use_global_device_ids=true | all-gather | bytes 1003520 | tf_op jit(solution)/shard_map/all_gather | solution.py:218
  35.7 0.0 copy-start.1
  35.7 0.0 copy-done.2
  35.7 1.1 %shard_map.73 = (bf16[1280,128]{1,0:T(8,128)(2,1)S(1)}, f32[4,15,128]{2,1,0:T(8,128)S(1)}) custom-call(bf16[4,784,128]{2,1,0:T(8,128)(2,1)S(1)} %bitcast.22, bf16[256,16,128]{2,1,0:T(8,128)(2,1)S(1)} %copy-done.2), custom_call_target="tpu_custom_call" | custom-call | flops 84000000 | bytes 2000000 | tf_op jit(solution)/shard_map/pallas_call | solution.py:150
  36.7 0.0 all-to-all-done
  36.7 1.2 %broadcast_in_dim.19 = bf16[4,1280,128]{2,1,0:T(8,128)(2,1)} broadcast(bf16[1280,128]{1,0:T(8,128)(2,1)S(1)} %get-tuple-element.13), dimensions={1,2} | broadcast | bytes 1638400 | tf_op jit(solution)/shard_map/broadcast_in_dim | solution.py:228
  38.0 0.0 copy-done.1
  38.0 4.3 %all-to-all-start.1 = ((bf16[4,1280,128]{2,1,0:T(8,128)(2,1)}), bf16[4,1280,128]{2,1,0:T(8,128)(2,1)}, u32[]{:S(2)}, u32[]{:S(2)}) async-start(bf16[4,1280,128]{2,1,0:T(8,128)(2,1)} %broadcast_in_dim.19), calls=%async_computation.1 | async-start | bytes 2621440 | tf_op jit(solution)/shard_map/all_to_all | solution.py:228
  42.3 6.8 %collective-permute-start = (bf16[2560,128]{1,0:T(8,128)(2,1)S(1)}, bf16[2560,128]{1,0:T(8,128)(2,1)S(1)}, u32[]{:S(2)}, u32[]{:S(2)}) collective-permute-start(bf16[2560,128]{1,0:T(8,128)(2,1)S(1)} %bitcast.24), channel_id=1, source_target_pairs={{0,4},{4,0},{1,5},{5,1},{2,6},{6,2},{3,7},{7,3},{8,12},{12,8},{9,1... | collective-permute-start | bytes 1966088 | tf_op jit(solution)/shard_map/ppermute | solution.py:230
  49.2 0.1 constant_dynamic-slice_fusion
  49.2 0.1 copy.10
  49.3 0.1 copy.13.coef_ref
  49.4 1.4 %collective-permute-done = bf16[2560,128]{1,0:T(8,128)(2,1)S(1)} collective-permute-done((bf16[2560,128]{1,0:T(8,128)(2,1)S(1)}, bf16[2560,128]{1,0:T(8,128)(2,1)S(1)}, u32[]{:S(2)}, u32[]{:S(2)}) %collective-permute-start) | collective-permute-done | bytes 655392 | tf_op jit(solution)/shard_map/ppermute | solution.py:230
  50.8 7.7 %shard_map.74 = (bf16[1024,2560]{1,0:T(8,128)(2,1)}, f32[8,128]{1,0:T(8,128)S(1)}) custom-call(f32[20,48]{1,0:T(8,128)S(1)} %copy.13.coef_ref, bf16[4,784,128]{2,1,0:T(8,128)(2,1)} %bitcast.23, bf16[160,16,128]{2,1,0:T(8,128)(2,1)S(1)} %bitcast.25, bf16[160,16,128]{2,1,0:T(8,128)(2,1)S(1)} %bitcast.26), custom_call_target="tpu_custom_call" | custom-call | flops 1500000000 | bytes 8000000 | tf_op jit(solution)/shard_map/pallas_call | solution.py:166
  58.5 0.0 all-to-all-done.1
  58.5 4.6 %collective-permute-start.1 = (bf16[4,1280,128]{2,1,0:T(8,128)(2,1)}, bf16[4,1280,128]{2,1,0:T(8,128)(2,1)S(1)}, u32[]{:S(2)}, u32[]{:S(2)}) collective-permute-start(bf16[4,1280,128]{2,1,0:T(8,128)(2,1)} %all-to-all-done.1), channel_id=1, source_target_pairs={{0,4},{4,0},{1,5},{5,1},{2,6},{6,2},{3,7},{7,3},{8,12},{12,8},{9,1... | collective-permute-start | bytes 3932168 | tf_op jit(solution)/shard_map/ppermute | solution.py:234
  63.1 2.9 %collective-permute-done.1 = bf16[4,1280,128]{2,1,0:T(8,128)(2,1)S(1)} collective-permute-done((bf16[4,1280,128]{2,1,0:T(8,128)(2,1)}, bf16[4,1280,128]{2,1,0:T(8,128)(2,1)S(1)}, u32[]{:S(2)}, u32[]{:S(2)}) %collective-permute-start.1) | collective-permute-done | bytes 1310752 | tf_op jit(solution)/shard_map/ppermute | solution.py:234
  66.0 0.0 copy-start.7
  66.0 1.1 %copy-done.7 = bf16[4,1280,128]{2,1,0:T(8,128)(2,1)} copy-done((bf16[4,1280,128]{2,1,0:T(8,128)(2,1)}, bf16[4,1280,128]{2,1,0:T(8,128)(2,1)S(1)}, u32[]{:S(2)}) %copy-start.7) | copy-done | bytes 1310744
  67.0 5.9 %shard_map.75 = bf16[4,16,4,16,128]{4,3,2,1,0:T(8,128)(2,1)S(1)} custom-call(bf16[1024,2560]{1,0:T(8,128)(2,1)} %get-tuple-element.15.frame_hbm, bf16[4,4,20,16,128]{4,3,2,1,0:T(8,128)(2,1)} %bitcast.13.mine_hbm, bf16[4,4,20,16,128]{4,3,2,1,0:T(8,128)(2,1)} %bitcast.34, f32[8,128]{1,0:T(8,128)S(1)} %get-tuple-element.18.token), custom_call_target="tpu_custom_call" | custom-call | flops 2700000000 | bytes 8000000 | tf_op jit(solution)/shard_map/pallas_call | solution.py:186
  73.0 16.0 %all_to_all.15 = bf16[4,16,4,16,128]{4,3,2,1,0:T(8,128)(2,1)S(1)} all-to-all(bf16[4,16,4,16,128]{4,3,2,1,0:T(8,128)(2,1)S(1)} %shard_map.75), channel_id=1, replica_groups=mesh['lrow'=8,'x1'=2,'x0'=2,'y'=2,'core'=2,'term'=4] {'x0','y'}, dimensions={0} | all-to-all | bytes 2097152 | tf_op jit(solution)/shard_map/all_to_all | solution.py:236
  88.9 0.0 copy-start.3
  88.9 0.2 convert_add_fusion
  89.1 0.9 copy-done.3
  90.0 1.0 %fusion = bf16[32,4,16,128]{3,2,1,0:T(8,128)(2,1)} fusion(f32[2,1,16,4,16,128]{5,4,3,2,1,0:T(8,128)S(1)} %convert_add_fusion, bf16[32,4,16,128]{3,2,1,0:T(8,128)(2,1)S(1)} %copy-done.3), kind=kLoop, calls=%fused_computation.1 | loop fusion | flops 786432 | bytes 2097152 | tf_op jit(solution)/shard_map/convert_element_type | solution.py:238
  (13 shorter events, 0.2 us)
Async XLA Ops:
  0.0 16.5 %copy-start = (bf16[5,256,256]{2,1,0:T(8,128)(2,1)S(1)}, bf16[5,256,256]{2,1,0:T(8,128)(2,1)}, u32[]{:S(2)}) copy-start(bf16[5,256,256]{2,1,0:T(8,128)(2,1)} %param.10) | copy-start | bytes 1966084
  1.4 14.9 %copy-start.4 = (f32[5,3,128]{2,1,0:T(4,128)S(1)}, f32[5,3,128]{2,1,0:T(4,128)}, u32[]{:S(2)}) copy-start(f32[5,3,128]{2,1,0:T(4,128)} %param.12) | copy-start | bytes 23044
  1.4 14.9 %copy-start.5 = (f32[5,3,128]{2,1,0:T(4,128)S(1)}, f32[5,3,128]{2,1,0:T(4,128)}, u32[]{:S(2)}) copy-start(f32[5,3,128]{2,1,0:T(4,128)} %param.11) | copy-start | bytes 23044
  1.4 15.0 %copy-start.6 = (bf16[5,4,256]{2,1,0:T(4,128)(2,1)S(1)}, bf16[5,4,256]{2,1,0:T(4,128)(2,1)}, u32[]{:S(2)}) copy-start(bf16[5,4,256]{2,1,0:T(4,128)(2,1)} %param.9) | copy-start | bytes 30724
  2.6 34.1 %all-to-all-start = ((bf16[32,80,128]{2,1,0:T(8,128)(2,1)}), bf16[32,80,128]{2,1,0:T(8,128)(2,1)S(1)}, u32[]{:S(2)}, u32[]{:S(2)}) async-start(bf16[32,80,128]{2,1,0:T(8,128)(2,1)} %bitcast.9), calls=%async_computation | async-start | bytes 1310720 | tf_op jit(solution)/shard_map/all_to_all | solution.py:225
  16.3 19.3 %copy-start.2 = (bf16[256,16,128]{2,1,0:T(8,128)(2,1)S(1)}, bf16[256,16,128]{2,1,0:T(8,128)(2,1)}, u32[]{:S(2)}) copy-start(bf16[256,16,128]{2,1,0:T(8,128)(2,1)} %core_ref.1) | copy-start | bytes 3145732
  35.7 2.3 %copy-start.1 = (bf16[3136,128]{1,0:T(8,128)(2,1)}, bf16[3136,128]{1,0:T(8,128)(2,1)S(1)}, u32[]{:S(2)}) copy-start(bf16[3136,128]{1,0:T(8,128)(2,1)S(1)} %all-gather) | copy-start | bytes 2408452
  38.0 20.5 %all-to-all-start.1 = ((bf16[4,1280,128]{2,1,0:T(8,128)(2,1)}), bf16[4,1280,128]{2,1,0:T(8,128)(2,1)}, u32[]{:S(2)}, u32[]{:S(2)}) async-start(bf16[4,1280,128]{2,1,0:T(8,128)(2,1)} %broadcast_in_dim.19), calls=%async_computation.1 | async-start | bytes 2621440 | tf_op jit(solution)/shard_map/all_to_all | solution.py:228
  42.3 8.5 %collective-permute-start = (bf16[2560,128]{1,0:T(8,128)(2,1)S(1)}, bf16[2560,128]{1,0:T(8,128)(2,1)S(1)}, u32[]{:S(2)}, u32[]{:S(2)}) collective-permute-start(bf16[2560,128]{1,0:T(8,128)(2,1)S(1)} %bitcast.24), channel_id=1, source_target_pairs={{0,4},{4,0},{1,5},{5,1},{2,6},{6,2},{3,7},{7,3},{8,12},{12,8},{9,1... | collective-permute-start | bytes 1966088 | tf_op jit(solution)/shard_map/ppermute | solution.py:230
  58.5 7.5 %collective-permute-start.1 = (bf16[4,1280,128]{2,1,0:T(8,128)(2,1)}, bf16[4,1280,128]{2,1,0:T(8,128)(2,1)S(1)}, u32[]{:S(2)}, u32[]{:S(2)}) collective-permute-start(bf16[4,1280,128]{2,1,0:T(8,128)(2,1)} %all-to-all-done.1), channel_id=1, source_target_pairs={{0,4},{4,0},{1,5},{5,1},{2,6},{6,2},{3,7},{7,3},{8,12},{12,8},{9,1... | collective-permute-start | bytes 3932168 | tf_op jit(solution)/shard_map/ppermute | solution.py:234
  66.0 1.1 %copy-start.7 = (bf16[4,1280,128]{2,1,0:T(8,128)(2,1)}, bf16[4,1280,128]{2,1,0:T(8,128)(2,1)S(1)}, u32[]{:S(2)}) copy-start(bf16[4,1280,128]{2,1,0:T(8,128)(2,1)S(1)} %collective-permute-done.1) | copy-start | bytes 3932164
  88.9 1.0 %copy-start.3 = (bf16[32,4,16,128]{3,2,1,0:T(8,128)(2,1)S(1)}, bf16[32,4,16,128]{3,2,1,0:T(8,128)(2,1)}, u32[]{:S(2)}) copy-start(bf16[32,4,16,128]{3,2,1,0:T(8,128)(2,1)} %param.13) | copy-start | bytes 1572868

commit v5 on v4

--- a/solution.py
+++ b/solution.py
@@ -86,18 +86,19 @@
         out(step).wait()
 
 
-def product_kernel(frame_hbm, mine_hbm, twin_hbm, token, out_ref, left_ref, frame, sem):
+def product_kernel(frame_hbm, mine_ref, twin_ref, projected_hbm, token, out_ref, kept_ref, left_ref, frame, sem):
+    keep = pltpu.make_async_copy(projected_hbm, kept_ref, sem.at[36])
     pieces = []
     for x in range(4):
         for a in range(4):
-            for move, source in enumerate((mine_hbm, twin_hbm)):
+            for move, source in enumerate((mine_ref, twin_ref)):
                 target = left_ref.at[:, pl.ds(move * 64 + x * 16, 16), pl.ds(a * 128, 128)]
                 pieces.append(pltpu.make_async_copy(source.at[x, a], target, sem.at[(x * 4 + a) * 2 + move]))
     chunks = [
         pltpu.make_async_copy(frame_hbm.at[pl.ds(at * 256, 256)], frame.at[pl.ds(at * 256, 256)], sem.at[32 + at])
         for at in range(4)
     ]
-    for copy in pieces + chunks:
+    for copy in pieces + chunks + [keep]:
         copy.start()
     for copy in pieces:
         copy.wait()
@@ -116,6 +117,7 @@
         return carry
 
     lax.fori_loop(0, 4, contract, 0)
+    keep.wait()
 
 
 def left_kernel(shared_ref, core_ref, out_ref, coef_ref, tall):
@@ -182,20 +184,23 @@
     )(coef, shared, mine, other)
 
 
-def product(frame, mine, twin, token):
+def product(frame, mine, twin, projected, token):
     return pl.pallas_call(
         product_kernel,
-        out_shape=jax.ShapeDtypeStruct((4, 16, 4, 16, 128), BF16),
-        in_specs=[HBM] + [ANYWHERE] * 3,
-        out_specs=VMEM,
+        out_shape=(
+            jax.ShapeDtypeStruct((4, 16, 4, 16, 128), BF16),
+            jax.ShapeDtypeStruct((32, 4, 16, 128), BF16),
+        ),
+        in_specs=[HBM, ANYWHERE, ANYWHERE, HBM, ANYWHERE],
+        out_specs=(VMEM, VMEM),
         scratch_shapes=[
             pltpu.VMEM((20, 128, 512), BF16),
             pltpu.VMEM((1024, 2560), BF16),
-            pltpu.SemaphoreType.DMA((36,)),
+            pltpu.SemaphoreType.DMA((37,)),
         ],
-        compiler_params=pltpu.CompilerParams(vmem_limit_bytes=52 << 20),
+        compiler_params=pltpu.CompilerParams(vmem_limit_bytes=46 << 20),
         cost_estimate=pl.CostEstimate(flops=2_700_000_000, bytes_accessed=8_000_000, transcendentals=0),
-    )(frame, mine, twin, token)
+    )(frame, mine, twin, projected, token)
 
 
 def on_device(core_left, core_right, env_left, env_right, coef_left, coef_right, projected):
@@ -232,10 +237,12 @@
     frame, token = right_frames(coef, shared, slices.reshape(160, 16, 128), other.reshape(160, 16, 128))
     token, lefts = lax.optimization_barrier((token, lefts))
     twins = lax.ppermute(lefts, "core", swap)
-    part = product(frame, lefts.reshape(4, 4, 20, 16, 128), twins.reshape(4, 4, 20, 16, 128), token)
+    part, kept = product(
+        frame, lefts.reshape(4, 4, 20, 16, 128), twins.reshape(4, 4, 20, 16, 128), projected, token
+    )
     part = lax.all_to_all(part, ("x0", "y"), 0, 0, tiled=True).reshape(2, 2, 16, 4, 16, 128)
     summed = (part[:, 0].astype(F32) + part[:, 1].astype(F32)).reshape(32, 4, 16, 128)
-    return (projected.astype(F32) - summed).astype(BF16)
+    return (kept.astype(F32) - summed).astype(BF16)
 
 
 def solution(mesh):

time: 91.6 us -> 88.5 us (0.966)
  local copies, waits for them, and re-layouts: 6.6 us -> 4.7 us
    unnamed x16 -> x14, local copies, waits for them, and re-layouts: 1.96 us -> 0.04 us
where the time goes in v5:
time: 88.5 us; the launch traced here: 88.1 us
  blocking collectives  34.5 us (39%)
  starting transfers between devices  28.9 us (33%)
  Pallas kernels  14.3 us (16%)
  local copies, waits for them, and re-layouts  4.7 us (5%)
  waiting for transfers between devices  4.18 us (5%)
  other arithmetic  1.19 us (1%)
    all_gather x1, blocking collectives, on_device(): shared = lax.all_gather(shared, 'term')  18.5 us
    all_to_all x1, blocking collectives, on_device(): lax.all_to_all(part, ('x0', 'y'), 0, 0, tiled=True)  16 us
    all_to_all x1, starting transfers between devices, on_device(): lax.all_to_all(windows, ('lrow', 'x1', 'x0'), 0, 0, tiled=True)  13.7 us
    pallas_call x1, Pallas kernels, right_frames(): pl.pallas_call(frames_kernel, out_shape=(jax.ShapeDtypeStruct((1024, 2560...  7.74 us
    ppermute x1, starting transfers between devices, on_device(): other = lax.ppermute(slices, 'core', swap)  7.05 us
    pallas_call x1, Pallas kernels, product(): pl.pallas_call(product_kernel, out_shape=(jax.ShapeDtypeStruct((4, 16, 4,...  5.49 us
    ppermute x1, starting transfers between devices, on_device(): twins = lax.ppermute(lefts, 'core', swap)  4.1 us
    all_to_all x1, starting transfers between devices, on_device(): lax.all_to_all(jnp.broadcast_to(left[None], (4, 1280, 128)), ('x1', 'x0')...  4.07 us
  transfers between devices with their start and end apart: 4, of which 2 were waited for; matrix products, arithmetic and copies ran while one was open for 1% of the time, Pallas kernels for 10%

profile of v5, /device:TPU:1, one launch (start us, length us, event | category | flops | bytes accessed | tf_op | source)
XLA Modules:
  0.0 88.1 jit_solution(7073243772001921133)
XLA Ops:
  0.0 0.0 copy-start
  0.0 1.1 %copy.13 = bf16[512,128]{0,1:T(8,128)(2,1)S(1)} copy(bf16[512,128]{1,0:T(8,128)(2,1)} %bitcast.39) | data formatting | bytes 262144 | tf_op jit(solution)/shard_map/reshape | solution.py:225
  1.1 0.1 stack.9
  1.3 0.1 stack.10
  1.4 0.0 copy-start.4
  1.4 0.0 copy-start.5
  1.4 0.0 copy-start.6
  1.4 0.1 copy.14
  1.5 0.1 broadcast_in_dim.17
  1.7 0.9 %broadcast_in_dim.18 = bf16[16,2,80,128]{3,2,1,0:T(8,128)(2,1)} broadcast(bf16[2,80,128]{2,1,0:T(8,128)(2,1)S(1)} %broadcast_in_dim.17), dimensions={1,2,3} | broadcast | bytes 696320 | tf_op jit(solution)/shard_map/broadcast_in_dim | solution.py:229
  2.6 13.7 %all-to-all-start = ((bf16[32,80,128]{2,1,0:T(8,128)(2,1)}), bf16[32,80,128]{2,1,0:T(8,128)(2,1)S(1)}, u32[]{:S(2)}, u32[]{:S(2)}) async-start(bf16[32,80,128]{2,1,0:T(8,128)(2,1)} %bitcast.9), calls=%async_computation | async-start | bytes 1310720 | tf_op jit(solution)/shard_map/all_to_all | solution.py:230
  16.3 0.0 copy-start.2
  16.3 0.0 copy-done.4
  16.4 0.0 copy-done.5
  16.4 0.0 copy-done.6
  16.5 0.0 copy-done
  16.5 0.6 concatenate.8
  17.1 18.5 %all-gather = bf16[3136,128]{1,0:T(8,128)(2,1)S(1)} all-gather(bf16[784,128]{1,0:T(8,128)(2,1)S(1)} %concatenate.8), channel_id=2, replica_groups=mesh['lrow'=8,'x1'=2,'x0'=2,'y'=2,'core'=2,'term'=4] {'term'}, dimensions={0}, use_global_device_ids=true | all-gather | bytes 1003520 | tf_op jit(solution)/shard_map/all_gather | solution.py:223
  35.7 0.0 copy-start.1
  35.7 0.0 copy-done.2
  35.7 1.1 %shard_map.73 = (bf16[1280,128]{1,0:T(8,128)(2,1)S(1)}, f32[4,15,128]{2,1,0:T(8,128)S(1)}) custom-call(bf16[4,784,128]{2,1,0:T(8,128)(2,1)S(1)} %bitcast.30, bf16[256,16,128]{2,1,0:T(8,128)(2,1)S(1)} %copy-done.2), custom_call_target="tpu_custom_call" | custom-call | flops 84000000 | bytes 2000000 | tf_op jit(solution)/shard_map/pallas_call | solution.py:152
  36.7 0.0 all-to-all-done
  36.7 1.3 %broadcast_in_dim.19 = bf16[4,1280,128]{2,1,0:T(8,128)(2,1)} broadcast(bf16[1280,128]{1,0:T(8,128)(2,1)S(1)} %get-tuple-element.15), dimensions={1,2} | broadcast | bytes 1638400 | tf_op jit(solution)/shard_map/broadcast_in_dim | solution.py:233
  38.0 0.0 copy-done.1
  38.0 4.1 %all-to-all-start.1 = ((bf16[4,1280,128]{2,1,0:T(8,128)(2,1)}), bf16[4,1280,128]{2,1,0:T(8,128)(2,1)S(1)}, u32[]{:S(2)}, u32[]{:S(2)}) async-start(bf16[4,1280,128]{2,1,0:T(8,128)(2,1)} %broadcast_in_dim.19), calls=%async_computation.1 | async-start | bytes 2621440 | tf_op jit(solution)/shard_map/all_to_all | solution.py:233
  42.1 7.1 %collective-permute-start = (bf16[2560,128]{1,0:T(8,128)(2,1)S(1)}, bf16[2560,128]{1,0:T(8,128)(2,1)}, u32[]{:S(2)}, u32[]{:S(2)}) collective-permute-start(bf16[2560,128]{1,0:T(8,128)(2,1)S(1)} %bitcast.33), channel_id=1, source_target_pairs={{0,4},{4,0},{1,5},{5,1},{2,6},{6,2},{3,7},{7,3},{8,12},{12,8},{9,1... | collective-permute-start | bytes 1966088 | tf_op jit(solution)/shard_map/ppermute | solution.py:235
  49.2 0.1 constant_dynamic-slice_fusion
  49.3 0.1 copy.12
  49.4 0.1 copy.15.coef_ref
  49.4 1.5 %collective-permute-done = bf16[2560,128]{1,0:T(8,128)(2,1)} collective-permute-done((bf16[2560,128]{1,0:T(8,128)(2,1)S(1)}, bf16[2560,128]{1,0:T(8,128)(2,1)}, u32[]{:S(2)}, u32[]{:S(2)}) %collective-permute-start) | collective-permute-done | bytes 655392 | tf_op jit(solution)/shard_map/ppermute | solution.py:235
  51.0 0.0 copy-start.3
  51.0 7.7 %shard_map.74 = (bf16[1024,2560]{1,0:T(8,128)(2,1)}, f32[8,128]{1,0:T(8,128)S(1)}) custom-call(f32[20,48]{1,0:T(8,128)S(1)} %copy.15.coef_ref, bf16[4,784,128]{2,1,0:T(8,128)(2,1)} %bitcast.31, bf16[160,16,128]{2,1,0:T(8,128)(2,1)S(1)} %bitcast.34, bf16[160,16,128]{2,1,0:T(8,128)(2,1)} %bitcast.12.other_hbm), custom_call_target="tpu_custom_call" | custom-call | flops 1500000000 | bytes 8000000 | tf_op jit(solution)/shard_map/pallas_call | solution.py:168
  58.7 0.0 all-to-all-done.1
  58.7 4.1 %collective-permute-start.1 = (bf16[4,1280,128]{2,1,0:T(8,128)(2,1)S(1)}, bf16[4,1280,128]{2,1,0:T(8,128)(2,1)S(1)}, u32[]{:S(2)}, u32[]{:S(2)}) collective-permute-start(bf16[4,1280,128]{2,1,0:T(8,128)(2,1)S(1)} %all-to-all-done.1), channel_id=1, source_target_pairs={{0,4},{4,0},{1,5},{5,1},{2,6},{6,2},{3,7},{7,3},{8,12},{12,8},{9,1... | collective-permute-start | bytes 3932168 | tf_op jit(solution)/shard_map/ppermute | solution.py:239
  62.9 2.6 %collective-permute-done.1 = bf16[4,1280,128]{2,1,0:T(8,128)(2,1)S(1)} collective-permute-done((bf16[4,1280,128]{2,1,0:T(8,128)(2,1)S(1)}, bf16[4,1280,128]{2,1,0:T(8,128)(2,1)S(1)}, u32[]{:S(2)}, u32[]{:S(2)}) %collective-permute-start.1) | collective-permute-done | bytes 1310752 | tf_op jit(solution)/shard_map/ppermute | solution.py:239
  65.5 0.0 copy-done.3
  65.5 5.5 %shard_map.75 = (bf16[4,16,4,16,128]{4,3,2,1,0:T(8,128)(2,1)S(1)}, bf16[32,4,16,128]{3,2,1,0:T(8,128)(2,1)S(1)}) custom-call(bf16[1024,2560]{1,0:T(8,128)(2,1)} %get-tuple-element.17.frame_hbm, bf16[4,4,20,16,128]{4,3,2,1,0:T(8,128)(2,1)S(1)} %bitcast.32, bf16[4,4,20,16,128]{4,3,2,1,0:T(8,128)(2,1)S(1)} %bitcast.35, bf16[32,4,16,128]{3,2,1,0:T(8,128)(2,1)S(1)} %copy-done.3, ...), custom_call_target="tpu_custom_call" | custom-call | flops 2700000000 | bytes 8000000 | tf_op jit(solution)/shard_map/pallas_call | solution.py:188
  71.0 16.0 %all_to_all.15 = bf16[4,16,4,16,128]{4,3,2,1,0:T(8,128)(2,1)S(1)} all-to-all(bf16[4,16,4,16,128]{4,3,2,1,0:T(8,128)(2,1)S(1)} %get-tuple-element.22), channel_id=1, replica_groups=mesh['lrow'=8,'x1'=2,'x0'=2,'y'=2,'core'=2,'term'=4] {'x0','y'}, dimensions={0} | all-to-all | bytes 2097152 | tf_op jit(solution)/shard_map/all_to_all | solution.py:243
  87.0 0.2 convert_add_fusion
  87.1 1.0 %fusion = bf16[32,4,16,128]{3,2,1,0:T(8,128)(2,1)} fusion(f32[2,1,16,4,16,128]{5,4,3,2,0,1:T(8,128)S(1)} %convert_add_fusion, bf16[32,4,16,128]{3,2,1,0:T(8,128)(2,1)S(1)} %get-tuple-element.21), kind=kLoop, calls=%fused_computation.1 | loop fusion | flops 786432 | bytes 2097152 | tf_op jit(solution)/shard_map/convert_element_type | solution.py:245
  (13 shorter events, 0.2 us)
Async XLA Ops:
  0.0 16.5 %copy-start = (bf16[5,256,256]{2,1,0:T(8,128)(2,1)S(1)}, bf16[5,256,256]{2,1,0:T(8,128)(2,1)}, u32[]{:S(2)}) copy-start(bf16[5,256,256]{2,1,0:T(8,128)(2,1)} %param.10) | copy-start | bytes 1966084
  1.4 14.9 %copy-start.4 = (f32[5,3,128]{2,1,0:T(4,128)S(1)}, f32[5,3,128]{2,1,0:T(4,128)}, u32[]{:S(2)}) copy-start(f32[5,3,128]{2,1,0:T(4,128)} %param.12) | copy-start | bytes 23044
  1.4 14.9 %copy-start.5 = (f32[5,3,128]{2,1,0:T(4,128)S(1)}, f32[5,3,128]{2,1,0:T(4,128)}, u32[]{:S(2)}) copy-start(f32[5,3,128]{2,1,0:T(4,128)} %param.11) | copy-start | bytes 23044
  1.4 15.0 %copy-start.6 = (bf16[5,4,256]{2,1,0:T(4,128)(2,1)S(1)}, bf16[5,4,256]{2,1,0:T(4,128)(2,1)}, u32[]{:S(2)}) copy-start(bf16[5,4,256]{2,1,0:T(4,128)(2,1)} %param.9) | copy-start | bytes 30724
  2.6 34.1 %all-to-all-start = ((bf16[32,80,128]{2,1,0:T(8,128)(2,1)}), bf16[32,80,128]{2,1,0:T(8,128)(2,1)S(1)}, u32[]{:S(2)}, u32[]{:S(2)}) async-start(bf16[32,80,128]{2,1,0:T(8,128)(2,1)} %bitcast.9), calls=%async_computation | async-start | bytes 1310720 | tf_op jit(solution)/shard_map/all_to_all | solution.py:230
  16.3 19.3 %copy-start.2 = (bf16[256,16,128]{2,1,0:T(8,128)(2,1)S(1)}, bf16[256,16,128]{2,1,0:T(8,128)(2,1)}, u32[]{:S(2)}) copy-start(bf16[256,16,128]{2,1,0:T(8,128)(2,1)} %core_ref.1) | copy-start | bytes 3145732
  35.7 2.4 %copy-start.1 = (bf16[3136,128]{1,0:T(8,128)(2,1)}, bf16[3136,128]{1,0:T(8,128)(2,1)S(1)}, u32[]{:S(2)}) copy-start(bf16[3136,128]{1,0:T(8,128)(2,1)S(1)} %all-gather) | copy-start | bytes 2408452
  38.0 20.7 %all-to-all-start.1 = ((bf16[4,1280,128]{2,1,0:T(8,128)(2,1)}), bf16[4,1280,128]{2,1,0:T(8,128)(2,1)S(1)}, u32[]{:S(2)}, u32[]{:S(2)}) async-start(bf16[4,1280,128]{2,1,0:T(8,128)(2,1)} %broadcast_in_dim.19), calls=%async_computation.1 | async-start | bytes 2621440 | tf_op jit(solution)/shard_map/all_to_all | solution.py:233
  42.1 8.9 %collective-permute-start = (bf16[2560,128]{1,0:T(8,128)(2,1)S(1)}, bf16[2560,128]{1,0:T(8,128)(2,1)}, u32[]{:S(2)}, u32[]{:S(2)}) collective-permute-start(bf16[2560,128]{1,0:T(8,128)(2,1)S(1)} %bitcast.33), channel_id=1, source_target_pairs={{0,4},{4,0},{1,5},{5,1},{2,6},{6,2},{3,7},{7,3},{8,12},{12,8},{9,1... | collective-permute-start | bytes 1966088 | tf_op jit(solution)/shard_map/ppermute | solution.py:235
  51.0 14.5 %copy-start.3 = (bf16[32,4,16,128]{3,2,1,0:T(8,128)(2,1)S(1)}, bf16[32,4,16,128]{3,2,1,0:T(8,128)(2,1)}, u32[]{:S(2)}) copy-start(bf16[32,4,16,128]{3,2,1,0:T(8,128)(2,1)} %projected_hbm.1) | copy-start | bytes 1572868
  58.7 6.7 %collective-permute-start.1 = (bf16[4,1280,128]{2,1,0:T(8,128)(2,1)S(1)}, bf16[4,1280,128]{2,1,0:T(8,128)(2,1)S(1)}, u32[]{:S(2)}, u32[]{:S(2)}) collective-permute-start(bf16[4,1280,128]{2,1,0:T(8,128)(2,1)S(1)} %all-to-all-done.1), channel_id=1, source_target_pairs={{0,4},{4,0},{1,5},{5,1},{2,6},{6,2},{3,7},{7,3},{8,12},{12,8},{9,1... | collective-permute-start | bytes 3932168 | tf_op jit(solution)/shard_map/ppermute | solution.py:239

commit v6 on v5

--- a/solution.py
+++ b/solution.py
@@ -145,7 +145,7 @@
         tall[pl.ds(r, 80, stride=16), :] = (
             centre * raw + lower * pltpu.roll(raw, 1, 1) + upper * pltpu.roll(raw, 127, 1)
         )
-    out_ref[...] = tall[...].astype(BF16)
+    out_ref[...] = tall[:1280].astype(BF16)
 
 
 def left_frames(shared, core):
@@ -154,7 +154,7 @@
         out_shape=(jax.ShapeDtypeStruct((1280, 128), BF16), jax.ShapeDtypeStruct((4, 15, 128), F32)),
         in_specs=[VMEM, VMEM],
         out_specs=(VMEM, VMEM),
-        scratch_shapes=[pltpu.VMEM((1280, 128), F32)],
+        scratch_shapes=[pltpu.VMEM((1296, 128), F32)],
         compiler_params=pltpu.CompilerParams(vmem_limit_bytes=8 << 20),
         cost_estimate=pl.CostEstimate(flops=84_000_000, bytes_accessed=2_000_000, transcendentals=0),
     )(shared, core)

time: 88.5 us -> 88.5 us (level)
  no operation moved by 1% of the time
where the time goes in v6:
time: 88.5 us; the launch traced here: 88.1 us
  blocking collectives  34.5 us (39%)
  starting transfers between devices  28.9 us (33%)
  Pallas kernels  14.3 us (16%)
  local copies, waits for them, and re-layouts  4.7 us (5%)
  waiting for transfers between devices  4.18 us (5%)
  other arithmetic  1.19 us (1%)
    all_gather x1, blocking collectives, on_device(): shared = lax.all_gather(shared, 'term')  18.5 us
    all_to_all x1, blocking collectives, on_device(): lax.all_to_all(part, ('x0', 'y'), 0, 0, tiled=True)  16 us
    all_to_all x1, starting transfers between devices, on_device(): lax.all_to_all(windows, ('lrow', 'x1', 'x0'), 0, 0, tiled=True)  13.7 us
    pallas_call x1, Pallas kernels, right_frames(): pl.pallas_call(frames_kernel, out_shape=(jax.ShapeDtypeStruct((1024, 2560...  7.74 us
    ppermute x1, starting transfers between devices, on_device(): other = lax.ppermute(slices, 'core', swap)  7.05 us
    pallas_call x1, Pallas kernels, product(): pl.pallas_call(product_kernel, out_shape=(jax.ShapeDtypeStruct((4, 16, 4,...  5.49 us
    ppermute x1, starting transfers between devices, on_device(): twins = lax.ppermute(lefts, 'core', swap)  4.1 us
    all_to_all x1, starting transfers between devices, on_device(): lax.all_to_all(jnp.broadcast_to(left[None], (4, 1280, 128)), ('x1', 'x0')...  4.07 us
  transfers between devices with their start and end apart: 4, of which 2 were waited for; matrix products, arithmetic and copies ran while one was open for 1% of the time, Pallas kernels for 10%

profile of v6, /device:TPU:1, one launch (start us, length us, event | category | flops | bytes accessed | tf_op | source)
XLA Modules:
  0.0 88.1 jit_solution(2492742203459295379)
XLA Ops:
  0.0 0.0 copy-start
  0.0 1.1 %copy.13 = bf16[512,128]{0,1:T(8,128)(2,1)S(1)} copy(bf16[512,128]{1,0:T(8,128)(2,1)} %bitcast.39) | data formatting | bytes 262144 | tf_op jit(solution)/shard_map/reshape | solution.py:225
  1.1 0.1 stack.9
  1.3 0.1 stack.10
  1.4 0.0 copy-start.4
  1.4 0.0 copy-start.5
  1.4 0.0 copy-start.6
  1.4 0.1 copy.14
  1.5 0.1 broadcast_in_dim.17
  1.7 0.9 %broadcast_in_dim.18 = bf16[16,2,80,128]{3,2,1,0:T(8,128)(2,1)} broadcast(bf16[2,80,128]{2,1,0:T(8,128)(2,1)S(1)} %broadcast_in_dim.17), dimensions={1,2,3} | broadcast | bytes 696320 | tf_op jit(solution)/shard_map/broadcast_in_dim | solution.py:229
  2.6 13.7 %all-to-all-start = ((bf16[32,80,128]{2,1,0:T(8,128)(2,1)}), bf16[32,80,128]{2,1,0:T(8,128)(2,1)S(1)}, u32[]{:S(2)}, u32[]{:S(2)}) async-start(bf16[32,80,128]{2,1,0:T(8,128)(2,1)} %bitcast.9), calls=%async_computation | async-start | bytes 1310720 | tf_op jit(solution)/shard_map/all_to_all | solution.py:230
  16.3 0.0 copy-start.2
  16.3 0.0 copy-done.4
  16.4 0.0 copy-done.5
  16.4 0.0 copy-done.6
  16.5 0.0 copy-done
  16.5 0.6 concatenate.8
  17.1 18.5 %all-gather = bf16[3136,128]{1,0:T(8,128)(2,1)S(1)} all-gather(bf16[784,128]{1,0:T(8,128)(2,1)S(1)} %concatenate.8), channel_id=2, replica_groups=mesh['lrow'=8,'x1'=2,'x0'=2,'y'=2,'core'=2,'term'=4] {'term'}, dimensions={0}, use_global_device_ids=true | all-gather | bytes 1003520 | tf_op jit(solution)/shard_map/all_gather | solution.py:223
  35.7 0.0 copy-start.1
  35.7 0.0 copy-done.2
  35.7 1.1 %shard_map.73 = (bf16[1280,128]{1,0:T(8,128)(2,1)S(1)}, f32[4,15,128]{2,1,0:T(8,128)S(1)}) custom-call(bf16[4,784,128]{2,1,0:T(8,128)(2,1)S(1)} %bitcast.30, bf16[256,16,128]{2,1,0:T(8,128)(2,1)S(1)} %copy-done.2), custom_call_target="tpu_custom_call" | custom-call | flops 84000000 | bytes 2000000 | tf_op jit(solution)/shard_map/pallas_call | solution.py:152
  36.7 0.0 all-to-all-done
  36.8 1.3 %broadcast_in_dim.19 = bf16[4,1280,128]{2,1,0:T(8,128)(2,1)} broadcast(bf16[1280,128]{1,0:T(8,128)(2,1)S(1)} %get-tuple-element.15), dimensions={1,2} | broadcast | bytes 1638400 | tf_op jit(solution)/shard_map/broadcast_in_dim | solution.py:233
  38.0 0.0 copy-done.1
  38.0 4.1 %all-to-all-start.1 = ((bf16[4,1280,128]{2,1,0:T(8,128)(2,1)}), bf16[4,1280,128]{2,1,0:T(8,128)(2,1)S(1)}, u32[]{:S(2)}, u32[]{:S(2)}) async-start(bf16[4,1280,128]{2,1,0:T(8,128)(2,1)} %broadcast_in_dim.19), calls=%async_computation.1 | async-start | bytes 2621440 | tf_op jit(solution)/shard_map/all_to_all | solution.py:233
  42.1 7.1 %collective-permute-start = (bf16[2560,128]{1,0:T(8,128)(2,1)S(1)}, bf16[2560,128]{1,0:T(8,128)(2,1)}, u32[]{:S(2)}, u32[]{:S(2)}) collective-permute-start(bf16[2560,128]{1,0:T(8,128)(2,1)S(1)} %bitcast.33), channel_id=1, source_target_pairs={{0,4},{4,0},{1,5},{5,1},{2,6},{6,2},{3,7},{7,3},{8,12},{12,8},{9,1... | collective-permute-start | bytes 1966088 | tf_op jit(solution)/shard_map/ppermute | solution.py:235
  49.2 0.1 constant_dynamic-slice_fusion
  49.3 0.1 copy.12
  49.4 0.1 copy.15.coef_ref
  49.4 1.5 %collective-permute-done = bf16[2560,128]{1,0:T(8,128)(2,1)} collective-permute-done((bf16[2560,128]{1,0:T(8,128)(2,1)S(1)}, bf16[2560,128]{1,0:T(8,128)(2,1)}, u32[]{:S(2)}, u32[]{:S(2)}) %collective-permute-start) | collective-permute-done | bytes 655392 | tf_op jit(solution)/shard_map/ppermute | solution.py:235
  51.0 0.0 copy-start.3
  51.0 7.7 %shard_map.74 = (bf16[1024,2560]{1,0:T(8,128)(2,1)}, f32[8,128]{1,0:T(8,128)S(1)}) custom-call(f32[20,48]{1,0:T(8,128)S(1)} %copy.15.coef_ref, bf16[4,784,128]{2,1,0:T(8,128)(2,1)} %bitcast.31, bf16[160,16,128]{2,1,0:T(8,128)(2,1)S(1)} %bitcast.34, bf16[160,16,128]{2,1,0:T(8,128)(2,1)} %bitcast.12.other_hbm), custom_call_target="tpu_custom_call" | custom-call | flops 1500000000 | bytes 8000000 | tf_op jit(solution)/shard_map/pallas_call | solution.py:168
  58.7 0.0 all-to-all-done.1
  58.7 4.1 %collective-permute-start.1 = (bf16[4,1280,128]{2,1,0:T(8,128)(2,1)S(1)}, bf16[4,1280,128]{2,1,0:T(8,128)(2,1)S(1)}, u32[]{:S(2)}, u32[]{:S(2)}) collective-permute-start(bf16[4,1280,128]{2,1,0:T(8,128)(2,1)S(1)} %all-to-all-done.1), channel_id=1, source_target_pairs={{0,4},{4,0},{1,5},{5,1},{2,6},{6,2},{3,7},{7,3},{8,12},{12,8},{9,1... | collective-permute-start | bytes 3932168 | tf_op jit(solution)/shard_map/ppermute | solution.py:239
  62.9 2.6 %collective-permute-done.1 = bf16[4,1280,128]{2,1,0:T(8,128)(2,1)S(1)} collective-permute-done((bf16[4,1280,128]{2,1,0:T(8,128)(2,1)S(1)}, bf16[4,1280,128]{2,1,0:T(8,128)(2,1)S(1)}, u32[]{:S(2)}, u32[]{:S(2)}) %collective-permute-start.1) | collective-permute-done | bytes 1310752 | tf_op jit(solution)/shard_map/ppermute | solution.py:239
  65.5 0.0 copy-done.3
  65.5 5.5 %shard_map.75 = (bf16[4,16,4,16,128]{4,3,2,1,0:T(8,128)(2,1)S(1)}, bf16[32,4,16,128]{3,2,1,0:T(8,128)(2,1)S(1)}) custom-call(bf16[1024,2560]{1,0:T(8,128)(2,1)} %get-tuple-element.17.frame_hbm, bf16[4,4,20,16,128]{4,3,2,1,0:T(8,128)(2,1)S(1)} %bitcast.32, bf16[4,4,20,16,128]{4,3,2,1,0:T(8,128)(2,1)S(1)} %bitcast.35, bf16[32,4,16,128]{3,2,1,0:T(8,128)(2,1)S(1)} %copy-done.3, ...), custom_call_target="tpu_custom_call" | custom-call | flops 2700000000 | bytes 8000000 | tf_op jit(solution)/shard_map/pallas_call | solution.py:188
  71.0 16.0 %all_to_all.15 = bf16[4,16,4,16,128]{4,3,2,1,0:T(8,128)(2,1)S(1)} all-to-all(bf16[4,16,4,16,128]{4,3,2,1,0:T(8,128)(2,1)S(1)} %get-tuple-element.22), channel_id=1, replica_groups=mesh['lrow'=8,'x1'=2,'x0'=2,'y'=2,'core'=2,'term'=4] {'x0','y'}, dimensions={0} | all-to-all | bytes 2097152 | tf_op jit(solution)/shard_map/all_to_all | solution.py:243
  87.0 0.2 convert_add_fusion
  87.1 1.0 %fusion = bf16[32,4,16,128]{3,2,1,0:T(8,128)(2,1)} fusion(f32[2,1,16,4,16,128]{5,4,3,2,0,1:T(8,128)S(1)} %convert_add_fusion, bf16[32,4,16,128]{3,2,1,0:T(8,128)(2,1)S(1)} %get-tuple-element.21), kind=kLoop, calls=%fused_computation.1 | loop fusion | flops 786432 | bytes 2097152 | tf_op jit(solution)/shard_map/convert_element_type | solution.py:245
  (13 shorter events, 0.2 us)
Async XLA Ops:
  0.0 16.5 %copy-start = (bf16[5,256,256]{2,1,0:T(8,128)(2,1)S(1)}, bf16[5,256,256]{2,1,0:T(8,128)(2,1)}, u32[]{:S(2)}) copy-start(bf16[5,256,256]{2,1,0:T(8,128)(2,1)} %param.10) | copy-start | bytes 1966084
  1.4 14.9 %copy-start.4 = (f32[5,3,128]{2,1,0:T(4,128)S(1)}, f32[5,3,128]{2,1,0:T(4,128)}, u32[]{:S(2)}) copy-start(f32[5,3,128]{2,1,0:T(4,128)} %param.12) | copy-start | bytes 23044
  1.4 14.9 %copy-start.5 = (f32[5,3,128]{2,1,0:T(4,128)S(1)}, f32[5,3,128]{2,1,0:T(4,128)}, u32[]{:S(2)}) copy-start(f32[5,3,128]{2,1,0:T(4,128)} %param.11) | copy-start | bytes 23044
  1.4 15.0 %copy-start.6 = (bf16[5,4,256]{2,1,0:T(4,128)(2,1)S(1)}, bf16[5,4,256]{2,1,0:T(4,128)(2,1)}, u32[]{:S(2)}) copy-start(bf16[5,4,256]{2,1,0:T(4,128)(2,1)} %param.9) | copy-start | bytes 30724
  2.6 34.1 %all-to-all-start = ((bf16[32,80,128]{2,1,0:T(8,128)(2,1)}), bf16[32,80,128]{2,1,0:T(8,128)(2,1)S(1)}, u32[]{:S(2)}, u32[]{:S(2)}) async-start(bf16[32,80,128]{2,1,0:T(8,128)(2,1)} %bitcast.9), calls=%async_computation | async-start | bytes 1310720 | tf_op jit(solution)/shard_map/all_to_all | solution.py:230
  16.3 19.3 %copy-start.2 = (bf16[256,16,128]{2,1,0:T(8,128)(2,1)S(1)}, bf16[256,16,128]{2,1,0:T(8,128)(2,1)}, u32[]{:S(2)}) copy-start(bf16[256,16,128]{2,1,0:T(8,128)(2,1)} %core_ref.1) | copy-start | bytes 3145732
  35.7 2.4 %copy-start.1 = (bf16[3136,128]{1,0:T(8,128)(2,1)}, bf16[3136,128]{1,0:T(8,128)(2,1)S(1)}, u32[]{:S(2)}) copy-start(bf16[3136,128]{1,0:T(8,128)(2,1)S(1)} %all-gather) | copy-start | bytes 2408452
  38.0 20.7 %all-to-all-start.1 = ((bf16[4,1280,128]{2,1,0:T(8,128)(2,1)}), bf16[4,1280,128]{2,1,0:T(8,128)(2,1)S(1)}, u32[]{:S(2)}, u32[]{:S(2)}) async-start(bf16[4,1280,128]{2,1,0:T(8,128)(2,1)} %broadcast_in_dim.19), calls=%async_computation.1 | async-start | bytes 2621440 | tf_op jit(solution)/shard_map/all_to_all | solution.py:233
  42.1 8.9 %collective-permute-start = (bf16[2560,128]{1,0:T(8,128)(2,1)S(1)}, bf16[2560,128]{1,0:T(8,128)(2,1)}, u32[]{:S(2)}, u32[]{:S(2)}) collective-permute-start(bf16[2560,128]{1,0:T(8,128)(2,1)S(1)} %bitcast.33), channel_id=1, source_target_pairs={{0,4},{4,0},{1,5},{5,1},{2,6},{6,2},{3,7},{7,3},{8,12},{12,8},{9,1... | collective-permute-start | bytes 1966088 | tf_op jit(solution)/shard_map/ppermute | solution.py:235
  51.0 14.5 %copy-start.3 = (bf16[32,4,16,128]{3,2,1,0:T(8,128)(2,1)S(1)}, bf16[32,4,16,128]{3,2,1,0:T(8,128)(2,1)}, u32[]{:S(2)}) copy-start(bf16[32,4,16,128]{3,2,1,0:T(8,128)(2,1)} %projected_hbm.1) | copy-start | bytes 1572868
  58.7 6.7 %collective-permute-start.1 = (bf16[4,1280,128]{2,1,0:T(8,128)(2,1)S(1)}, bf16[4,1280,128]{2,1,0:T(8,128)(2,1)S(1)}, u32[]{:S(2)}, u32[]{:S(2)}) collective-permute-start(bf16[4,1280,128]{2,1,0:T(8,128)(2,1)S(1)} %all-to-all-done.1), channel_id=1, source_target_pairs={{0,4},{4,0},{1,5},{5,1},{2,6},{6,2},{3,7},{7,3},{8,12},{12,8},{9,1... | collective-permute-start | bytes 3932168 | tf_op jit(solution)/shard_map/ppermute | solution.py:239

commit v7 on v6

--- a/solution.py
+++ b/solution.py
@@ -95,8 +95,8 @@
                 target = left_ref.at[:, pl.ds(move * 64 + x * 16, 16), pl.ds(a * 128, 128)]
                 pieces.append(pltpu.make_async_copy(source.at[x, a], target, sem.at[(x * 4 + a) * 2 + move]))
     chunks = [
-        pltpu.make_async_copy(frame_hbm.at[pl.ds(at * 256, 256)], frame.at[pl.ds(at * 256, 256)], sem.at[32 + at])
-        for at in range(4)
+        pltpu.make_async_copy(frame_hbm.at[pl.ds(at * 512, 512)], frame.at[pl.ds(at * 512, 512)], sem.at[32 + at])
+        for at in range(2)
     ]
     for copy in pieces + chunks + [keep]:
         copy.start()
@@ -104,19 +104,19 @@
         copy.wait()
 
     def contract(step, carry):
-        start = pl.multiple_of(step * 256, 256)
-        pltpu.make_async_copy(frame_hbm.at[pl.ds(start, 256)], frame.at[pl.ds(start, 256)], sem.at[32 + step]).wait()
+        start = pl.multiple_of(step * 512, 512)
+        pltpu.make_async_copy(frame_hbm.at[pl.ds(start, 512)], frame.at[pl.ds(start, 512)], sem.at[32 + step]).wait()
         part = jnp.dot(
-            frame[pl.ds(start, 256), :], left_ref[...].reshape(2560, 512), preferred_element_type=F32
+            frame[pl.ds(start, 512), :], left_ref[...].reshape(2560, 512), preferred_element_type=F32
         ).astype(BF16)
-        for at in range(4):
+        for at in range(8):
             for dest in range(4):
                 top = at * 64 + dest * 16
                 for a in range(4):
-                    out_ref[dest, step * 4 + at, a] = part[top : top + 16, a * 128 : (a + 1) * 128]
+                    out_ref[dest, step * 8 + at, a] = part[top : top + 16, a * 128 : (a + 1) * 128]
         return carry
 
-    lax.fori_loop(0, 4, contract, 0)
+    lax.fori_loop(0, 2, contract, 0)
     keep.wait()
 
 

time: 88.5 us -> 88.6 us (level)
  no operation moved by 1% of the time
where the time goes in v7:
time: 88.6 us; the launch traced here: 88.2 us
  blocking collectives  34.5 us (39%)
  starting transfers between devices  28.9 us (33%)
  Pallas kernels  14.4 us (16%)
  local copies, waits for them, and re-layouts  4.7 us (5%)
  waiting for transfers between devices  4.18 us (5%)
  other arithmetic  1.19 us (1%)
    all_gather x1, blocking collectives, on_device(): shared = lax.all_gather(shared, 'term')  18.5 us
    all_to_all x1, blocking collectives, on_device(): lax.all_to_all(part, ('x0', 'y'), 0, 0, tiled=True)  16 us
    all_to_all x1, starting transfers between devices, on_device(): lax.all_to_all(windows, ('lrow', 'x1', 'x0'), 0, 0, tiled=True)  13.7 us
    pallas_call x1, Pallas kernels, right_frames(): pl.pallas_call(frames_kernel, out_shape=(jax.ShapeDtypeStruct((1024, 2560...  7.74 us
    ppermute x1, starting transfers between devices, on_device(): other = lax.ppermute(slices, 'core', swap)  7.05 us
    pallas_call x1, Pallas kernels, product(): pl.pallas_call(product_kernel, out_shape=(jax.ShapeDtypeStruct((4, 16, 4,...  5.58 us
    ppermute x1, starting transfers between devices, on_device(): twins = lax.ppermute(lefts, 'core', swap)  4.1 us
    all_to_all x1, starting transfers between devices, on_device(): lax.all_to_all(jnp.broadcast_to(left[None], (4, 1280, 128)), ('x1', 'x0')...  4.07 us
  transfers between devices with their start and end apart: 4, of which 2 were waited for; matrix products, arithmetic and copies ran while one was open for 1% of the time, Pallas kernels for 10%

profile of v7, /device:TPU:1, one launch (start us, length us, event | category | flops | bytes accessed | tf_op | source)
XLA Modules:
  0.0 88.2 jit_solution(15359079919954917716)
XLA Ops:
  0.0 0.0 copy-start
  0.0 1.1 %copy.13 = bf16[512,128]{0,1:T(8,128)(2,1)S(1)} copy(bf16[512,128]{1,0:T(8,128)(2,1)} %bitcast.39) | data formatting | bytes 262144 | tf_op jit(solution)/shard_map/reshape | solution.py:225
  1.1 0.1 stack.9
  1.3 0.1 stack.10
  1.4 0.0 copy-start.4
  1.4 0.0 copy-start.5
  1.4 0.0 copy-start.6
  1.4 0.1 copy.14
  1.5 0.1 broadcast_in_dim.17
  1.7 0.9 %broadcast_in_dim.18 = bf16[16,2,80,128]{3,2,1,0:T(8,128)(2,1)} broadcast(bf16[2,80,128]{2,1,0:T(8,128)(2,1)S(1)} %broadcast_in_dim.17), dimensions={1,2,3} | broadcast | bytes 696320 | tf_op jit(solution)/shard_map/broadcast_in_dim | solution.py:229
  2.6 13.7 %all-to-all-start = ((bf16[32,80,128]{2,1,0:T(8,128)(2,1)}), bf16[32,80,128]{2,1,0:T(8,128)(2,1)S(1)}, u32[]{:S(2)}, u32[]{:S(2)}) async-start(bf16[32,80,128]{2,1,0:T(8,128)(2,1)} %bitcast.9), calls=%async_computation | async-start | bytes 1310720 | tf_op jit(solution)/shard_map/all_to_all | solution.py:230
  16.3 0.0 copy-start.2
  16.3 0.0 copy-done.4
  16.4 0.0 copy-done.5
  16.4 0.0 copy-done.6
  16.5 0.0 copy-done
  16.5 0.6 concatenate.8
  17.1 18.5 %all-gather = bf16[3136,128]{1,0:T(8,128)(2,1)S(1)} all-gather(bf16[784,128]{1,0:T(8,128)(2,1)S(1)} %concatenate.8), channel_id=2, replica_groups=mesh['lrow'=8,'x1'=2,'x0'=2,'y'=2,'core'=2,'term'=4] {'term'}, dimensions={0}, use_global_device_ids=true | all-gather | bytes 1003520 | tf_op jit(solution)/shard_map/all_gather | solution.py:223
  35.7 0.0 copy-start.1
  35.7 0.0 copy-done.2
  35.7 1.1 %shard_map.73 = (bf16[1280,128]{1,0:T(8,128)(2,1)S(1)}, f32[4,15,128]{2,1,0:T(8,128)S(1)}) custom-call(bf16[4,784,128]{2,1,0:T(8,128)(2,1)S(1)} %bitcast.30, bf16[256,16,128]{2,1,0:T(8,128)(2,1)S(1)} %copy-done.2), custom_call_target="tpu_custom_call" | custom-call | flops 84000000 | bytes 2000000 | tf_op jit(solution)/shard_map/pallas_call | solution.py:152
  36.7 0.0 all-to-all-done
  36.8 1.3 %broadcast_in_dim.19 = bf16[4,1280,128]{2,1,0:T(8,128)(2,1)} broadcast(bf16[1280,128]{1,0:T(8,128)(2,1)S(1)} %get-tuple-element.15), dimensions={1,2} | broadcast | bytes 1638400 | tf_op jit(solution)/shard_map/broadcast_in_dim | solution.py:233
  38.0 0.0 copy-done.1
  38.0 4.1 %all-to-all-start.1 = ((bf16[4,1280,128]{2,1,0:T(8,128)(2,1)}), bf16[4,1280,128]{2,1,0:T(8,128)(2,1)S(1)}, u32[]{:S(2)}, u32[]{:S(2)}) async-start(bf16[4,1280,128]{2,1,0:T(8,128)(2,1)} %broadcast_in_dim.19), calls=%async_computation.1 | async-start | bytes 2621440 | tf_op jit(solution)/shard_map/all_to_all | solution.py:233
  42.1 7.1 %collective-permute-start = (bf16[2560,128]{1,0:T(8,128)(2,1)S(1)}, bf16[2560,128]{1,0:T(8,128)(2,1)}, u32[]{:S(2)}, u32[]{:S(2)}) collective-permute-start(bf16[2560,128]{1,0:T(8,128)(2,1)S(1)} %bitcast.33), channel_id=1, source_target_pairs={{0,4},{4,0},{1,5},{5,1},{2,6},{6,2},{3,7},{7,3},{8,12},{12,8},{9,1... | collective-permute-start | bytes 1966088 | tf_op jit(solution)/shard_map/ppermute | solution.py:235
  49.2 0.1 constant_dynamic-slice_fusion
  49.3 0.1 copy.12
  49.4 0.1 copy.15.coef_ref
  49.4 1.5 %collective-permute-done = bf16[2560,128]{1,0:T(8,128)(2,1)} collective-permute-done((bf16[2560,128]{1,0:T(8,128)(2,1)S(1)}, bf16[2560,128]{1,0:T(8,128)(2,1)}, u32[]{:S(2)}, u32[]{:S(2)}) %collective-permute-start) | collective-permute-done | bytes 655392 | tf_op jit(solution)/shard_map/ppermute | solution.py:235
  51.0 0.0 copy-start.3
  51.0 7.7 %shard_map.74 = (bf16[1024,2560]{1,0:T(8,128)(2,1)}, f32[8,128]{1,0:T(8,128)S(1)}) custom-call(f32[20,48]{1,0:T(8,128)S(1)} %copy.15.coef_ref, bf16[4,784,128]{2,1,0:T(8,128)(2,1)} %bitcast.31, bf16[160,16,128]{2,1,0:T(8,128)(2,1)S(1)} %bitcast.34, bf16[160,16,128]{2,1,0:T(8,128)(2,1)} %bitcast.12.other_hbm), custom_call_target="tpu_custom_call" | custom-call | flops 1500000000 | bytes 8000000 | tf_op jit(solution)/shard_map/pallas_call | solution.py:168
  58.7 0.0 all-to-all-done.1
  58.7 4.1 %collective-permute-start.1 = (bf16[4,1280,128]{2,1,0:T(8,128)(2,1)S(1)}, bf16[4,1280,128]{2,1,0:T(8,128)(2,1)S(1)}, u32[]{:S(2)}, u32[]{:S(2)}) collective-permute-start(bf16[4,1280,128]{2,1,0:T(8,128)(2,1)S(1)} %all-to-all-done.1), channel_id=1, source_target_pairs={{0,4},{4,0},{1,5},{5,1},{2,6},{6,2},{3,7},{7,3},{8,12},{12,8},{9,1... | collective-permute-start | bytes 3932168 | tf_op jit(solution)/shard_map/ppermute | solution.py:239
  62.9 2.6 %collective-permute-done.1 = bf16[4,1280,128]{2,1,0:T(8,128)(2,1)S(1)} collective-permute-done((bf16[4,1280,128]{2,1,0:T(8,128)(2,1)S(1)}, bf16[4,1280,128]{2,1,0:T(8,128)(2,1)S(1)}, u32[]{:S(2)}, u32[]{:S(2)}) %collective-permute-start.1) | collective-permute-done | bytes 1310752 | tf_op jit(solution)/shard_map/ppermute | solution.py:239
  65.5 0.0 copy-done.3
  65.5 5.6 %shard_map.75 = (bf16[4,16,4,16,128]{4,3,2,1,0:T(8,128)(2,1)S(1)}, bf16[32,4,16,128]{3,2,1,0:T(8,128)(2,1)S(1)}) custom-call(bf16[1024,2560]{1,0:T(8,128)(2,1)} %get-tuple-element.17.frame_hbm, bf16[4,4,20,16,128]{4,3,2,1,0:T(8,128)(2,1)S(1)} %bitcast.32, bf16[4,4,20,16,128]{4,3,2,1,0:T(8,128)(2,1)S(1)} %bitcast.35, bf16[32,4,16,128]{3,2,1,0:T(8,128)(2,1)S(1)} %copy-done.3, ...), custom_call_target="tpu_custom_call" | custom-call | flops 2700000000 | bytes 8000000 | tf_op jit(solution)/shard_map/pallas_call | solution.py:188
  71.1 16.0 %all_to_all.15 = bf16[4,16,4,16,128]{4,3,2,1,0:T(8,128)(2,1)S(1)} all-to-all(bf16[4,16,4,16,128]{4,3,2,1,0:T(8,128)(2,1)S(1)} %get-tuple-element.22), channel_id=1, replica_groups=mesh['lrow'=8,'x1'=2,'x0'=2,'y'=2,'core'=2,'term'=4] {'x0','y'}, dimensions={0} | all-to-all | bytes 2097152 | tf_op jit(solution)/shard_map/all_to_all | solution.py:243
  87.0 0.2 convert_add_fusion
  87.2 1.0 %fusion = bf16[32,4,16,128]{3,2,1,0:T(8,128)(2,1)} fusion(f32[2,1,16,4,16,128]{5,4,3,2,0,1:T(8,128)S(1)} %convert_add_fusion, bf16[32,4,16,128]{3,2,1,0:T(8,128)(2,1)S(1)} %get-tuple-element.21), kind=kLoop, calls=%fused_computation.1 | loop fusion | flops 786432 | bytes 2097152 | tf_op jit(solution)/shard_map/convert_element_type | solution.py:245
  (13 shorter events, 0.2 us)
Async XLA Ops:
  0.0 16.5 %copy-start = (bf16[5,256,256]{2,1,0:T(8,128)(2,1)S(1)}, bf16[5,256,256]{2,1,0:T(8,128)(2,1)}, u32[]{:S(2)}) copy-start(bf16[5,256,256]{2,1,0:T(8,128)(2,1)} %param.10) | copy-start | bytes 1966084
  1.4 14.9 %copy-start.4 = (f32[5,3,128]{2,1,0:T(4,128)S(1)}, f32[5,3,128]{2,1,0:T(4,128)}, u32[]{:S(2)}) copy-start(f32[5,3,128]{2,1,0:T(4,128)} %param.12) | copy-start | bytes 23044
  1.4 14.9 %copy-start.5 = (f32[5,3,128]{2,1,0:T(4,128)S(1)}, f32[5,3,128]{2,1,0:T(4,128)}, u32[]{:S(2)}) copy-start(f32[5,3,128]{2,1,0:T(4,128)} %param.11) | copy-start | bytes 23044
  1.4 15.0 %copy-start.6 = (bf16[5,4,256]{2,1,0:T(4,128)(2,1)S(1)}, bf16[5,4,256]{2,1,0:T(4,128)(2,1)}, u32[]{:S(2)}) copy-start(bf16[5,4,256]{2,1,0:T(4,128)(2,1)} %param.9) | copy-start | bytes 30724
  2.6 34.1 %all-to-all-start = ((bf16[32,80,128]{2,1,0:T(8,128)(2,1)}), bf16[32,80,128]{2,1,0:T(8,128)(2,1)S(1)}, u32[]{:S(2)}, u32[]{:S(2)}) async-start(bf16[32,80,128]{2,1,0:T(8,128)(2,1)} %bitcast.9), calls=%async_computation | async-start | bytes 1310720 | tf_op jit(solution)/shard_map/all_to_all | solution.py:230
  16.3 19.3 %copy-start.2 = (bf16[256,16,128]{2,1,0:T(8,128)(2,1)S(1)}, bf16[256,16,128]{2,1,0:T(8,128)(2,1)}, u32[]{:S(2)}) copy-start(bf16[256,16,128]{2,1,0:T(8,128)(2,1)} %core_ref.1) | copy-start | bytes 3145732
  35.7 2.4 %copy-start.1 = (bf16[3136,128]{1,0:T(8,128)(2,1)}, bf16[3136,128]{1,0:T(8,128)(2,1)S(1)}, u32[]{:S(2)}) copy-start(bf16[3136,128]{1,0:T(8,128)(2,1)S(1)} %all-gather) | copy-start | bytes 2408452
  38.0 20.7 %all-to-all-start.1 = ((bf16[4,1280,128]{2,1,0:T(8,128)(2,1)}), bf16[4,1280,128]{2,1,0:T(8,128)(2,1)S(1)}, u32[]{:S(2)}, u32[]{:S(2)}) async-start(bf16[4,1280,128]{2,1,0:T(8,128)(2,1)} %broadcast_in_dim.19), calls=%async_computation.1 | async-start | bytes 2621440 | tf_op jit(solution)/shard_map/all_to_all | solution.py:233
  42.1 8.9 %collective-permute-start = (bf16[2560,128]{1,0:T(8,128)(2,1)S(1)}, bf16[2560,128]{1,0:T(8,128)(2,1)}, u32[]{:S(2)}, u32[]{:S(2)}) collective-permute-start(bf16[2560,128]{1,0:T(8,128)(2,1)S(1)} %bitcast.33), channel_id=1, source_target_pairs={{0,4},{4,0},{1,5},{5,1},{2,6},{6,2},{3,7},{7,3},{8,12},{12,8},{9,1... | collective-permute-start | bytes 1966088 | tf_op jit(solution)/shard_map/ppermute | solution.py:235
  51.0 14.5 %copy-start.3 = (bf16[32,4,16,128]{3,2,1,0:T(8,128)(2,1)S(1)}, bf16[32,4,16,128]{3,2,1,0:T(8,128)(2,1)}, u32[]{:S(2)}) copy-start(bf16[32,4,16,128]{3,2,1,0:T(8,128)(2,1)} %projected_hbm.1) | copy-start | bytes 1572868
  58.7 6.7 %collective-permute-start.1 = (bf16[4,1280,128]{2,1,0:T(8,128)(2,1)S(1)}, bf16[4,1280,128]{2,1,0:T(8,128)(2,1)S(1)}, u32[]{:S(2)}, u32[]{:S(2)}) collective-permute-start(bf16[4,1280,128]{2,1,0:T(8,128)(2,1)S(1)} %all-to-all-done.1), channel_id=1, source_target_pairs={{0,4},{4,0},{1,5},{5,1},{2,6},{6,2},{3,7},{7,3},{8,12},{12,8},{9,1... | collective-permute-start | bytes 3932168 | tf_op jit(solution)/shard_map/ppermute | solution.py:239
